TPU v7x, 128 devices: a whole 4x4x4 slice. The times are simulated.
128 devices in a mesh: gx: 4 (over z), gy: 4 (over x), gz: 8 (over y, core).
Axes of the slice: x: 4, y: 4, z: 4, core: 2. Of those that a mesh axis runs over, the one named last changes fastest.
Arguments:
- orbitals: float32 [32, 32, 32, 1024], P(None, 'gx', 'gy', 'gz'), may hold values from -6 to 6
- potential: float32 [32, 32, 1024], P('gx', 'gy', 'gz'), may hold values from -2 to 0
- projectors: float32 [1024, 4, 512], P(('gx', 'gy', 'gz')), may hold values from -0.5 to 0.5
- owner_rank: int32 [1024], replicated, may hold values from 0 to 127, as said below
- box_anchor: int32 [3, 1024], replicated, may hold values from 0 to 120, as said below
- box_extent: int32 [1024], replicated, may hold values from 4 to 8
- coupling: float32 [1024, 4], replicated, may hold values from 0.5 to 3
Outputs:
- filtered: float32 [32, 32, 32, 1024], P(None, 'gx', 'gy', 'gz')
- intersection: float32 [32, 32], replicated
Inputs may be any that keep to these rules, and one draw needn't show every extreme that they name: owner_rank[a] is (ix * 4 + iy) * 8 + iz for the domain (ix, iy, iz) that holds all of atom a's box; every device holds at most 24 atoms, an eighth of the devices exactly 24. box_anchor[0, a] is at most 0, box_anchor[1, a] at most 0, box_anchor[2, a] at most 120, so each box lies inside its owner's domain.
All inputs are finite; a program needn't handle non-finite values.
Results may differ from a plain program's by a relative error of at most 0.00013.
Values sent between devices are 32-bit elements; how exact they have to be, the bound alone decides.
A program may use at most 128 MiB of HBM per device.

v0:
```python
import jax
import jax.numpy as jnp
from jax import lax
from jax.sharding import PartitionSpec as P

B = 8
DEGREE = 4
ATOM_DEV = 8


STENCIL = (
    -5369.0 / 1800.0,
    12.0 / 7.0,
    -15.0 / 56.0,
    10.0 / 189.0,
    -1.0 / 112.0,
    2.0 / 1925.0,
    -1.0 / 16632.0,
)
SPACING = 0.5
LOW_EDGE = -2.5
CUTOFF = 4.0
UPPER = 60.0


def extended(cells, sides, width):
    for axis, dim in sides:
        count = lax.axis_size(axis)
        head = lax.slice_in_dim(cells, 0, width, axis=dim)
        tail = lax.slice_in_dim(cells, cells.shape[dim] - width, cells.shape[dim], axis=dim)
        cells = jnp.concatenate(
            [
                lax.ppermute(tail, axis, [(i, (i + 1) % count) for i in range(count)]),
                cells,
                lax.ppermute(head, axis, [((i + 1) % count, i) for i in range(count)]),
            ],
            axis=dim,
        )
    return cells


def laplace_padded(padded, shape):
    span_x, span_y, span_z = (shape[1], shape[2], shape[3])
    summed = 3.0 * STENCIL[0] * padded[:, 6 : 6 + span_x, 6 : 6 + span_y, 6 : 6 + span_z]
    for offset in range(1, 7):
        weight = STENCIL[offset]
        summed = summed + weight * (
            padded[:, 6 + offset : 6 + offset + span_x, 6 : 6 + span_y, 6 : 6 + span_z]
            + padded[:, 6 - offset : 6 - offset + span_x, 6 : 6 + span_y, 6 : 6 + span_z]
        )
        summed = summed + weight * (
            padded[:, 6 : 6 + span_x, 6 + offset : 6 + offset + span_y, 6 : 6 + span_z]
            + padded[:, 6 : 6 + span_x, 6 - offset : 6 - offset + span_y, 6 : 6 + span_z]
        )
        summed = summed + weight * (
            padded[:, 6 : 6 + span_x, 6 : 6 + span_y, 6 + offset : 6 + offset + span_z]
            + padded[:, 6 : 6 + span_x, 6 : 6 + span_y, 6 - offset : 6 - offset + span_z]
        )
    return summed / (SPACING * SPACING)


def collect_boxes(projectors, member, box_anchor, box_extent, coupling, capacity):
    member_int = member.astype(jnp.int32)
    slot_all = jnp.cumsum(member_int) - 1
    count = jnp.sum(member_int)
    slot_ids = jnp.arange(capacity, dtype=jnp.int32)
    onehot = ((slot_all[None, :] == slot_ids[:, None]) & member[None, :]).astype(jnp.float32)
    buffer = jnp.einsum(
        "cp,pkf->ckf",
        onehot,
        lax.all_gather(projectors, ("gx", "gy", "gz"), axis=0, tiled=True),
        precision=lax.Precision.HIGHEST,
    )
    hot_all = (slot_all[None, :] == slot_ids[:, None]) & member[None, :]
    slot_anchor = jnp.sum(jnp.where(hot_all[None, :, :], box_anchor[:, None, :], 0), axis=2)
    slot_extent = jnp.sum(jnp.where(hot_all, box_extent[None, :], 0), axis=1)
    slot_coupling = jnp.sum(jnp.where(hot_all[:, :, None], coupling[None, :, :], 0.0), axis=1)
    cell_offsets = jnp.arange(B, dtype=jnp.int32)
    limit = slot_extent[:, None, None, None]
    inside = (
        (cell_offsets[None, :, None, None] < limit)
        & (cell_offsets[None, None, :, None] < limit)
        & (cell_offsets[None, None, None, :] < limit)
    )
    buffer = buffer * inside.reshape(capacity, 1, B * B * B).astype(jnp.float32)
    return (buffer, slot_anchor, slot_coupling, count)


def nonlocal_term(field, buffer, slot_anchor, slot_coupling, count, domain_start):
    states = field.shape[0]

    def add_slot(slot_index, nonlocal_sum):
        corner = slot_anchor[:, slot_index] - domain_start
        start_cell = (0, corner[0], corner[1], corner[2])
        box_cells = lax.dynamic_slice(field, start_cell, (states, B, B, B)).reshape(
            states, B * B * B
        )
        proj_box = buffer[slot_index]
        coeffs = (
            jnp.dot(box_cells, proj_box.T, precision=lax.Precision.HIGHEST)
            * slot_coupling[slot_index][None, :]
        )
        addition = jnp.dot(coeffs, proj_box, precision=lax.Precision.HIGHEST).reshape(
            states, B, B, B
        )
        current = lax.dynamic_slice(nonlocal_sum, start_cell, (states, B, B, B))
        return lax.dynamic_update_slice(nonlocal_sum, current + addition, start_cell)

    return lax.fori_loop(0, count, add_slot, jnp.zeros_like(field))


def run_filter(field, apply_h):
    half_width = (UPPER - CUTOFF) / 2.0
    middle = (UPPER + CUTOFF) / 2.0
    sigma_one = half_width / (LOW_EDGE - middle)
    sigma_now = sigma_one
    result = (apply_h(field) - middle * field) * (sigma_one / half_width)
    previous = field
    for degree_step in range(1, DEGREE):
        sigma_next = 1.0 / (2.0 / sigma_one - sigma_now)
        next_state = (apply_h(result) - middle * result) * (
            2.0 * sigma_next / half_width
        ) - sigma_now * sigma_next * previous
        previous = result
        result = next_state
        sigma_now = sigma_next
    return result


def body(orbitals, potential, projectors, owner_rank, box_anchor, box_extent, coupling):
    groups_y = lax.axis_size("gy")
    groups_z = lax.axis_size("gz")
    own_x = owner_rank // (groups_y * groups_z)
    own_y = owner_rank // groups_z % groups_y
    own_z = owner_rank % groups_z
    index_x = lax.axis_index("gx")
    index_y = lax.axis_index("gy")
    index_z = lax.axis_index("gz")
    span_x, span_y, span_z = (orbitals.shape[1], orbitals.shape[2], orbitals.shape[3])
    grid_anchor = jnp.stack([own_x * span_x, own_y * span_y, own_z * span_z]) + box_anchor
    member = (own_x == index_x) & (own_y == index_y) & (own_z == index_z)
    buffer, slot_anchor, slot_coupling, count = collect_boxes(
        projectors, member, grid_anchor, box_extent, coupling, 3 * ATOM_DEV
    )
    domain_start = jnp.stack([index_x * span_x, index_y * span_y, index_z * span_z])

    def apply_cube(field):
        padded = extended(field, (("gx", 1), ("gy", 2), ("gz", 3)), 6)
        return (
            -0.5 * laplace_padded(padded, field.shape)
            + potential[None] * field
            + nonlocal_term(field, buffer, slot_anchor, slot_coupling, count, domain_start)
        )

    filtered = run_filter(orbitals, apply_cube)
    flattened = filtered.reshape(filtered.shape[0], -1)
    partial_value = jnp.dot(flattened, flattened.T, precision=lax.Precision.HIGHEST)
    cells_total = span_x * span_y * span_z * lax.axis_size("gx") * groups_y * groups_z
    intersection = lax.psum(partial_value, ("gx", "gy", "gz")) / cells_total
    return (filtered, intersection)


def solution(mesh):
    return jax.shard_map(
        body,
        mesh=mesh,
        in_specs=(
            P(None, "gx", "gy", "gz"),
            P("gx", "gy", "gz"),
            P(("gx", "gy", "gz"), None, None),
            P(),
            P(),
            P(),
            P(),
        ),
        out_specs=(P(None, "gx", "gy", "gz"), P()),
        check_vma=False,
    )
```

profile of v0, /device:TPU:1, one launch (start us, length us, event | category | flops | bytes accessed | tf_op | source)
XLA Modules:
  0.0 1504.8 jit_solution(13709826803225961729)
XLA Ops:
  15.5 17.2 %collective-permute-done.1 = f32[32,6,8,128]{3,0,2,1:T(8,128)} collective-permute-done((f32[32,6,8,128]{3,0,2,1:T(8,128)S(1)}, f32[32,6,8,128]{3,0,2,1:T(8,128)}, u32[]{:S(2)}, u32[]{:S(2)}) %collective-permute-start.1) | collective-permute-done | bytes 786464 | tf_op jit(solution)/shard_map/ppermute | solution.py:33
  49.3 50.0 %collective-permute-done.2 = f32[32,20,6,128]{3,0,2,1:T(8,128)} collective-permute-done((f32[32,20,6,128]{3,0,2,1:T(8,128)}, f32[32,20,6,128]{3,0,2,1:T(8,128)}, u32[]{:S(2)}, u32[]{:S(2)}) %collective-permute-start.2) | collective-permute-done | bytes 1966112 | tf_op jit(solution)/shard_map/ppermute | solution.py:35
  108.7 11.4 fusion.277
  136.5 8.9 collective-permute-done.5
  169.6 232.7 %while.40 = (s32[]{:T(128)}, f32[32,8,8,128]{0,3,2,1:T(8,128)}, s32[]{:T(128)}, s32[3,24]{0,1:T(8,128)S(1)}, s32[3]{0:T(128)S(1)}, /*index=5*/f32[32,8,8,128]{0,...) while((s32[]{:T(128)}, f32[32,8,8,128]{0,3,2,1:T(8,128)}, ...), condition=%wide.region_7.8_spmd, body=%wide.region_6.7_spmd.sunk | while | flops 1589387 | bytes 509233 | solution.py:109
  405.2 25.3 %broadcast_multiply_fusion = (f32[32,8,8,128]{3,0,2,1:T(8,128)S(1)}, f32[32,8,8,128]{3,0,2,1:T(8,128)}) fusion(f32[32,8,8,128]{3,0,2,1:T(8,128)S(1)} %copy.108, f32[8,8,128]{2,1,0:T(8,128)S(1)} %copy-done.10, f32[32,20,6,128]{3,0,2,1:T(8,128)} %collective-permute-done.2, f32[32,20,8,128]{3,0,2,1:T(8,128)} %copy-done, ...), kind=kLoop, calls=%fused_computation.473 | loop fusion | flops 28835840 | bytes 23977984 | tf_op jit(solution)/shard_map/mul | solution.py:117
  436.0 15.5 %collective-permute-done.6 = f32[32,6,8,128]{3,0,2,1:T(8,128)S(1)} collective-permute-done((f32[32,6,8,128]{3,0,2,1:T(8,128)}, f32[32,6,8,128]{3,0,2,1:T(8,128)S(1)}, u32[]{:S(2)}, u32[]{:S(2)}) %collective-permute-start.6) | collective-permute-done | bytes 786464 | tf_op jit(solution)/shard_map/ppermute | solution.py:35
  460.6 236.7 %while.41 = (s32[]{:T(128)}, f32[32,8,8,128]{0,3,2,1:T(8,128)}, s32[]{:T(128)}, s32[3,24]{0,1:T(8,128)S(1)}, s32[3]{0:T(128)S(1)}, /*index=5*/f32[32,8,8,128]{0,...) while((s32[]{:T(128)}, f32[32,8,8,128]{0,3,2,1:T(8,128)}, ...), condition=%wide.region_9.10_spmd, body=%wide.region_8.9_spmd.sunk | while | flops 1589387 | bytes 509233 | solution.py:109
  705.7 11.4 fusion.276
  717.1 6.5 copy.110
  724.4 6.5 copy.112
  754.2 16.3 %fusion.134 = f32[32,8,8,128]{3,0,2,1:T(8,128)S(1)} fusion(f32[32,8,8,128]{3,0,2,1:T(8,128)} %copy.118, f32[32,8,8,128]{3,0,2,1:T(8,128)S(1)} %get-tuple-element.374, f32[32,6,8,128]{3,0,2,1:T(8,128)} %collective-permute-done.7, f32[32,6,8,128]{3,0,2,1:T(8,128)} %copy-done.8, f32[32,20,20,6]{3,0,2,1:T(8,128)} %copy.113, ...), kind=kLoop, calls=%fused_computation.253 | loop fusion | flops 35651584 | bytes 23977984 | tf_op jit(solution)/shard_map/sub | solution.py:121
  775.7 12.5 collective-permute-done.12
  795.9 224.6 %while.42 = (s32[]{:T(128)}, f32[32,8,8,128]{0,3,2,1:T(8,128)}, s32[]{:T(128)}, s32[3,24]{0,1:T(8,128)S(1)}, s32[3]{0:T(128)S(1)}, /*index=5*/f32[32,8,8,128]{0,...) while((s32[]{:T(128)}, f32[32,8,8,128]{0,3,2,1:T(8,128)}, ...), condition=%wide.region_11.12_spmd, body=%wide.region_10.11_spmd.sunk | while | flops 1589387 | bytes 509233 | solution.py:109
  1029.4 11.4 fusion.275
  1040.7 6.5 copy.120
  1050.9 6.5 copy.122
  1079.7 15.6 %fusion.90 = f32[32,8,8,128]{3,0,2,1:T(8,128)S(1)} fusion(f32[32,8,8,128]{3,0,2,1:T(8,128)} %copy.128, f32[32,8,8,128]{3,0,2,1:T(8,128)S(1)} %fusion.134, f32[32,6,8,128]{3,0,2,1:T(8,128)} %copy-done.7, f32[32,6,8,128]{3,0,2,1:T(8,128)S(1)} %copy-done.6, f32[32,20,20,6]{3,0,2,1:T(8,128)} %copy.123, f32[32,20,6,128]{3,0,2,1:T(8,128)} %copy-done.4, ...), kind=kLoop, calls=%fused_computation.209 | loop fusion | flops 35651584 | bytes 22929408 | tf_op jit(solution)/shard_map/sub | solution.py:121
  1100.9 11.6 collective-permute-done.18
  1121.7 232.5 %while.43 = (s32[]{:T(128)}, f32[32,8,8,128]{0,3,2,1:T(8,128)}, s32[]{:T(128)}, s32[3,24]{0,1:T(8,128)S(1)}, s32[3]{0:T(128)S(1)}, /*index=5*/f32[32,8,8,128]{0,...) while((s32[]{:T(128)}, f32[32,8,8,128]{0,3,2,1:T(8,128)}, ...), condition=%wide.region_13.14_spmd, body=%wide.region_12.13_spmd.sunk | while | flops 1589387 | bytes 509233 | solution.py:109
  1362.7 11.4 fusion.274
  1385.2 6.5 copy.131
  1414.0 15.3 %fusion.46 = f32[32,8,8,128]{3,0,2,1:T(8,128)S(1)} fusion(f32[32,8,8,128]{3,0,2,1:T(8,128)} %copy.137, f32[32,8,8,128]{3,0,2,1:T(8,128)S(1)} %fusion.90, f32[32,6,8,128]{3,0,2,1:T(8,128)} %collective-permute-done.19, f32[32,6,8,128]{3,0,2,1:T(8,128)S(1)} %collective-permute-done.18, f32[32,20,20,6]{3,0,2,1:T(8,128)} %copy.132, ...), kind=kLoop, calls=%fused_computation.165 | loop fusion | flops 35651584 | bytes 22929408 | tf_op jit(solution)/shard_map/sub | solution.py:121
  1431.9 65.2 %psum.7 = f32[32,32]{1,0:T(8,128)S(1)} all-reduce(f32[32,32]{1,0:T(8,128)S(1)} %convolution_bitcast_fusion), channel_id=1, replica_groups=mesh['gx'=4,'gy'=4,'gz'=8] {'gx','gy','gz'}, use_global_device_ids=true, to_apply=%region_14.15 | all-reduce | flops 1024 | bytes 8192 | tf_op jit(solution)/shard_map/psum | solution.py:159
  (1012 shorter events, 908.7 us)
Async XLA Ops:
  7.2 152.9 %all-gather.2.cloned.1.call-start = ((), (), s32[]{:S(2)}) async-start(), calls=%async_computation | async-start | bytes 8454144 | tf_op jit(solution)/shard_map/all_gather | solution.py:71
  10.5 22.2 %collective-permute-start.1 = (f32[32,6,8,128]{3,0,2,1:T(8,128)S(1)}, f32[32,6,8,128]{3,0,2,1:T(8,128)}, u32[]{:S(2)}, u32[]{:S(2)}) collective-permute-start(f32[32,6,8,128]{3,0,2,1:T(8,128)S(1)} %copy.157), channel_id=1, source_target_pairs={{0,32},{32,64},{64,96},{96,0},{1,33},{33,65},{65,97},{97,1},{2,34}... | collective-permute-start | bytes 2359304 | tf_op jit(solution)/shard_map/ppermute | solution.py:33
  13.3 22.6 %collective-permute-start = (f32[32,6,8,128]{3,0,2,1:T(8,128)S(1)}, f32[32,6,8,128]{3,0,2,1:T(8,128)}, u32[]{:S(2)}, u32[]{:S(2)}) collective-permute-start(f32[32,6,8,128]{3,0,2,1:T(8,128)S(1)} %copy.158), channel_id=1, source_target_pairs={{32,0},{64,32},{96,64},{0,96},{33,1},{65,33},{97,65},{1,97},{34,2}... | collective-permute-start | bytes 2359304 | tf_op jit(solution)/shard_map/ppermute | solution.py:35
  41.7 57.6 %collective-permute-start.2 = (f32[32,20,6,128]{3,0,2,1:T(8,128)}, f32[32,20,6,128]{3,0,2,1:T(8,128)}, u32[]{:S(2)}, u32[]{:S(2)}) collective-permute-start(f32[32,20,6,128]{3,0,2,1:T(8,128)} %get-tuple-element.399), channel_id=1, source_target_pairs={{8,0},{16,8},{24,16},{0,24},{9,1},{17,9},{25,17},{1,25},{10,2},{18... | collective-permute-start | bytes 5898248 | tf_op jit(solution)/shard_map/ppermute | solution.py:35
  44.2 58.6 %collective-permute-start.3 = (f32[32,20,6,128]{3,0,2,1:T(8,128)}, f32[32,20,6,128]{3,0,2,1:T(8,128)}, u32[]{:S(2)}, u32[]{:S(2)}) collective-permute-start(f32[32,20,6,128]{3,0,2,1:T(8,128)} %get-tuple-element.398), channel_id=1, source_target_pairs={{0,8},{8,16},{16,24},{24,0},{1,9},{9,17},{17,25},{25,1},{2,10},{10... | collective-permute-start | bytes 5898248 | tf_op jit(solution)/shard_map/ppermute | solution.py:33
  126.2 19.1 %collective-permute-start.5 = (f32[32,20,20,6]{0,2,3,1:T(8,128)S(1)}, f32[32,20,20,6]{0,2,3,1:T(8,128)S(1)}, u32[]{:S(2)}, u32[]{:S(2)}) collective-permute-start(f32[32,20,20,6]{0,2,3,1:T(8,128)S(1)} %copy.99), channel_id=1, source_target_pairs={{0,1},{1,2},{2,3},{3,4},{4,5},{5,6},{6,7},{7,0},{8,9},{9,10},{10,1... | collective-permute-start | bytes 921608 | tf_op jit(solution)/shard_map/ppermute | solution.py:33
  135.5 19.1 %collective-permute-start.4 = (f32[32,20,20,6]{0,2,3,1:T(8,128)}, f32[32,20,20,6]{0,2,3,1:T(8,128)}, u32[]{:S(2)}, u32[]{:S(2)}) collective-permute-start(f32[32,20,20,6]{0,2,3,1:T(8,128)} %copy.97), channel_id=1, source_target_pairs={{1,0},{2,1},{3,2},{4,3},{5,4},{6,5},{7,6},{0,7},{9,8},{10,9},{11,1... | collective-permute-start | bytes 921608 | tf_op jit(solution)/shard_map/ppermute | solution.py:35
  431.9 19.7 %collective-permute-start.6 = (f32[32,6,8,128]{3,0,2,1:T(8,128)}, f32[32,6,8,128]{3,0,2,1:T(8,128)S(1)}, u32[]{:S(2)}, u32[]{:S(2)}) collective-permute-start(f32[32,6,8,128]{3,0,2,1:T(8,128)} %get-tuple-element.404), channel_id=1, source_target_pairs={{32,0},{64,32},{96,64},{0,96},{33,1},{65,33},{97,65},{1,97},{34,2}... | collective-permute-start | bytes 2359304 | tf_op jit(solution)/shard_map/ppermute | solution.py:35
  431.9 20.9 %collective-permute-start.7 = (f32[32,6,8,128]{3,0,2,1:T(8,128)}, f32[32,6,8,128]{3,0,2,1:T(8,128)}, u32[]{:S(2)}, u32[]{:S(2)}) collective-permute-start(f32[32,6,8,128]{3,0,2,1:T(8,128)} %get-tuple-element.405), channel_id=1, source_target_pairs={{0,32},{32,64},{64,96},{96,0},{1,33},{33,65},{65,97},{97,1},{2,34}... | collective-permute-start | bytes 2359304 | tf_op jit(solution)/shard_map/ppermute | solution.py:33
  456.6 244.4 %collective-permute-start.8 = (f32[32,20,6,128]{3,0,2,1:T(8,128)}, f32[32,20,6,128]{3,0,2,1:T(8,128)}, u32[]{:S(2)}, u32[]{:S(2)}) collective-permute-start(f32[32,20,6,128]{3,0,2,1:T(8,128)} %get-tuple-element.397), channel_id=1, source_target_pairs={{8,0},{16,8},{24,16},{0,24},{9,1},{17,9},{25,17},{1,25},{10,2},{18... | collective-permute-start | bytes 5898248 | tf_op jit(solution)/shard_map/ppermute | solution.py:35
  456.6 244.4 %collective-permute-start.9 = (f32[32,20,6,128]{3,0,2,1:T(8,128)}, f32[32,20,6,128]{3,0,2,1:T(8,128)}, u32[]{:S(2)}, u32[]{:S(2)}) collective-permute-start(f32[32,20,6,128]{3,0,2,1:T(8,128)} %get-tuple-element.396), channel_id=1, source_target_pairs={{0,8},{8,16},{16,24},{24,0},{1,9},{9,17},{17,25},{25,1},{2,10},{10... | collective-permute-start | bytes 5898248 | tf_op jit(solution)/shard_map/ppermute | solution.py:33
  723.6 19.4 %collective-permute-start.10 = (f32[32,20,20,6]{0,2,3,1:T(8,128)}, f32[32,20,20,6]{0,2,3,1:T(8,128)}, u32[]{:S(2)}, u32[]{:S(2)}) collective-permute-start(f32[32,20,20,6]{0,2,3,1:T(8,128)} %copy.110), channel_id=1, source_target_pairs={{1,0},{2,1},{3,2},{4,3},{5,4},{6,5},{7,6},{0,7},{9,8},{10,9},{11,1... | collective-permute-start | bytes 921608 | tf_op jit(solution)/shard_map/ppermute | solution.py:35
  730.9 17.6 %collective-permute-start.11 = (f32[32,20,20,6]{0,2,3,1:T(8,128)}, f32[32,20,20,6]{0,2,3,1:T(8,128)}, u32[]{:S(2)}, u32[]{:S(2)}) collective-permute-start(f32[32,20,20,6]{0,2,3,1:T(8,128)} %copy.112), channel_id=1, source_target_pairs={{0,1},{1,2},{2,3},{3,4},{4,5},{5,6},{6,7},{7,0},{8,9},{9,10},{10,1... | collective-permute-start | bytes 921608 | tf_op jit(solution)/shard_map/ppermute | solution.py:33
  771.5 16.6 %collective-permute-start.12 = (f32[32,6,8,128]{3,0,2,1:T(8,128)}, f32[32,6,8,128]{3,0,2,1:T(8,128)S(1)}, u32[]{:S(2)}, u32[]{:S(2)}) collective-permute-start(f32[32,6,8,128]{3,0,2,1:T(8,128)} %get-tuple-element.402), channel_id=1, source_target_pairs={{32,0},{64,32},{96,64},{0,96},{33,1},{65,33},{97,65},{1,97},{34,2}... | collective-permute-start | bytes 2359304 | tf_op jit(solution)/shard_map/ppermute | solution.py:35
  771.5 17.6 %collective-permute-start.13 = (f32[32,6,8,128]{3,0,2,1:T(8,128)S(1)}, f32[32,6,8,128]{3,0,2,1:T(8,128)S(1)}, u32[]{:S(2)}, u32[]{:S(2)}) collective-permute-start(f32[32,6,8,128]{3,0,2,1:T(8,128)S(1)} %get-tuple-element.403), channel_id=1, source_target_pairs={{0,32},{32,64},{64,96},{96,0},{1,33},{33,65},{65,97},{97,1},{2,34}... | collective-permute-start | bytes 2359304 | tf_op jit(solution)/shard_map/ppermute | solution.py:33
  791.8 232.2 %collective-permute-start.14 = (f32[32,20,6,128]{3,0,2,1:T(8,128)}, f32[32,20,6,128]{3,0,2,1:T(8,128)S(1)}, u32[]{:S(2)}, u32[]{:S(2)}) collective-permute-start(f32[32,20,6,128]{3,0,2,1:T(8,128)} %get-tuple-element.393), channel_id=1, source_target_pairs={{8,0},{16,8},{24,16},{0,24},{9,1},{17,9},{25,17},{1,25},{10,2},{18... | collective-permute-start | bytes 5898248 | tf_op jit(solution)/shard_map/ppermute | solution.py:35
  791.9 232.2 %collective-permute-start.15 = (f32[32,20,6,128]{3,0,2,1:T(8,128)}, f32[32,20,6,128]{3,0,2,1:T(8,128)}, u32[]{:S(2)}, u32[]{:S(2)}) collective-permute-start(f32[32,20,6,128]{3,0,2,1:T(8,128)} %get-tuple-element.392), channel_id=1, source_target_pairs={{0,8},{8,16},{16,24},{24,0},{1,9},{9,17},{17,25},{25,1},{2,10},{10... | collective-permute-start | bytes 5898248 | tf_op jit(solution)/shard_map/ppermute | solution.py:33
  1047.2 19.4 %collective-permute-start.16 = (f32[32,20,20,6]{0,2,3,1:T(8,128)}, f32[32,20,20,6]{0,2,3,1:T(8,128)}, u32[]{:S(2)}, u32[]{:S(2)}) collective-permute-start(f32[32,20,20,6]{0,2,3,1:T(8,128)} %copy.120), channel_id=1, source_target_pairs={{1,0},{2,1},{3,2},{4,3},{5,4},{6,5},{7,6},{0,7},{9,8},{10,9},{11,1... | collective-permute-start | bytes 921608 | tf_op jit(solution)/shard_map/ppermute | solution.py:35
  1057.4 16.6 %collective-permute-start.17 = (f32[32,20,20,6]{0,2,3,1:T(8,128)}, f32[32,20,20,6]{0,2,3,1:T(8,128)}, u32[]{:S(2)}, u32[]{:S(2)}) collective-permute-start(f32[32,20,20,6]{0,2,3,1:T(8,128)} %copy.122), channel_id=1, source_target_pairs={{0,1},{1,2},{2,3},{3,4},{4,5},{5,6},{6,7},{7,0},{8,9},{9,10},{10,1... | collective-permute-start | bytes 921608 | tf_op jit(solution)/shard_map/ppermute | solution.py:33
  1096.8 16.9 %collective-permute-start.19 = (f32[32,6,8,128]{3,0,2,1:T(8,128)}, f32[32,6,8,128]{3,0,2,1:T(8,128)}, u32[]{:S(2)}, u32[]{:S(2)}) collective-permute-start(f32[32,6,8,128]{3,0,2,1:T(8,128)} %get-tuple-element.401), channel_id=1, source_target_pairs={{0,32},{32,64},{64,96},{96,0},{1,33},{33,65},{65,97},{97,1},{2,34}... | collective-permute-start | bytes 2359304 | tf_op jit(solution)/shard_map/ppermute | solution.py:33
  1117.5 240.3 %collective-permute-start.20 = (f32[32,20,6,128]{3,0,2,1:T(8,128)}, f32[32,20,6,128]{3,0,2,1:T(8,128)}, u32[]{:S(2)}, u32[]{:S(2)}) collective-permute-start(f32[32,20,6,128]{3,0,2,1:T(8,128)} %get-tuple-element.389), channel_id=1, source_target_pairs={{8,0},{16,8},{24,16},{0,24},{9,1},{17,9},{25,17},{1,25},{10,2},{18... | collective-permute-start | bytes 5898248 | tf_op jit(solution)/shard_map/ppermute | solution.py:35
  1117.5 240.3 %collective-permute-start.21 = (f32[32,20,6,128]{3,0,2,1:T(8,128)}, f32[32,20,6,128]{3,0,2,1:T(8,128)}, u32[]{:S(2)}, u32[]{:S(2)}) collective-permute-start(f32[32,20,6,128]{3,0,2,1:T(8,128)} %get-tuple-element.388), channel_id=1, source_target_pairs={{0,8},{8,16},{16,24},{24,0},{1,9},{9,17},{17,25},{25,1},{2,10},{10... | collective-permute-start | bytes 5898248 | tf_op jit(solution)/shard_map/ppermute | solution.py:33
  1380.5 19.4 %collective-permute-start.22 = (f32[32,20,20,6]{0,2,3,1:T(8,128)}, f32[32,20,20,6]{0,2,3,1:T(8,128)}, u32[]{:S(2)}, u32[]{:S(2)}) collective-permute-start(f32[32,20,20,6]{0,2,3,1:T(8,128)} %copy.129), channel_id=1, source_target_pairs={{1,0},{2,1},{3,2},{4,3},{5,4},{6,5},{7,6},{0,7},{9,8},{10,9},{11,1... | collective-permute-start | bytes 921608 | tf_op jit(solution)/shard_map/ppermute | solution.py:35
  1391.8 16.6 %collective-permute-start.23 = (f32[32,20,20,6]{0,2,3,1:T(8,128)}, f32[32,20,20,6]{0,2,3,1:T(8,128)}, u32[]{:S(2)}, u32[]{:S(2)}) collective-permute-start(f32[32,20,20,6]{0,2,3,1:T(8,128)} %copy.131), channel_id=1, source_target_pairs={{0,1},{1,2},{2,3},{3,4},{4,5},{5,6},{6,7},{7,0},{8,9},{9,10},{10,1... | collective-permute-start | bytes 921608 | tf_op jit(solution)/shard_map/ppermute | solution.py:33
  (16 other events, 173.4 us)
Sparse Core Ops, SparseCore 0:
  11.6 81.3 all-gather.1
where the time goes:
time: 1530 us; the launch traced here: 1500 us
  local copies, waits for them, and re-layouts  626 us (41%)
  matrix products  260 us (17%)
  loops' own time  250 us (16%)
  waiting for transfers between devices  142 us (9%)
  other arithmetic  117 us (8%)
  blocking collectives  65.2 us (4%)
  starting transfers between devices  29.3 us (2%)
    another operation x4, loops' own time, nonlocal_term(): return lax.fori_loop(0, count, add_slot, jnp.zeros_like(field))  250 us
    dynamic_update_slice x96, local copies, waits for them, and re-layouts, add_slot(): lax.dynamic_update_slice(nonlocal_sum, current + addition, start_cell)  182 us
    dot_general x96, matrix products, add_slot(): jnp.dot(coeffs, proj_box, precision=lax.Precision.HIGHEST)  162 us
    dynamic_slice x96, local copies, waits for them, and re-layouts, add_slot(): lax.dynamic_slice(field, start_cell, (states, B, B, B))  105 us
    ppermute x12, waiting for transfers between devices, extended(): lax.ppermute(head, axis, [((i + 1) % count, i) for i in range(count)])  105 us
    dot_general x96, matrix products, add_slot(): jnp.dot(box_cells, proj_box.T, precision=lax.Precision.HIGHEST)  90.7 us
    dot_general x192, local copies, waits for them, and re-layouts, add_slot(): jnp.dot(coeffs, proj_box, precision=lax.Precision.HIGHEST)  78.2 us
    slice x12, local copies, waits for them, and re-layouts, extended(): head = lax.slice_in_dim(cells, 0, width, axis=dim)  76.8 us
  transfers between devices with their start and end apart: 25, of which 16 were waited for; matrix products, arithmetic and copies ran while one was open for 43% of the time, Pallas kernels for 0%

commit v1 on v0

v1 whole, which is shorter than its diff:
```python
import functools

import jax
import jax.numpy as jnp
import numpy as np
from jax import lax
from jax.experimental import pallas as pl
from jax.experimental.pallas import tpu as pltpu
from jax.sharding import PartitionSpec as P

B = 8
DEGREE = 4
STENCIL = (
    -5369.0 / 1800.0,
    12.0 / 7.0,
    -15.0 / 56.0,
    10.0 / 189.0,
    -1.0 / 112.0,
    2.0 / 1925.0,
    -1.0 / 16632.0,
)
SPACING = 0.5
LOW_EDGE = -2.5
CUTOFF = 4.0
UPPER = 60.0
HALF = (UPPER - CUTOFF) / 2.0
MIDDLE = (UPPER + CUTOFF) / 2.0

G = 16
PAD = 40
ROWS = 208
HALO = 32
MARGIN = 27
RANGES = ((16, 176), (24, 160), (32, 144), (40, 128))
WSCALE = 35.0 / 32.0
KIN = -0.5 / (SPACING * SPACING)
DIAG = KIN * 3.0 * STENCIL[0] - MIDDLE
SLOTS = 1040
F32 = jnp.float32
BF16 = jnp.bfloat16


def steps():
    sigma_one = HALF / (LOW_EDGE - MIDDLE)
    sigma = sigma_one
    out = [(sigma_one / HALF, 0.0)]
    for _ in range(1, DEGREE):
        nxt = 1.0 / (2.0 / sigma_one - sigma)
        out.append((2.0 * nxt / HALF, sigma * nxt))
        sigma = nxt
    return out


def weights():
    c = np.asarray(STENCIL, np.float64) * WSCALE

    def coef(m):
        m = abs(m)
        return c[m] if 1 <= m <= 6 else 0.0

    eye = np.eye(8)
    band = {s: np.array([[coef(8 * s + a - b) for b in range(8)] for a in range(8)]) for s in (-1, 0, 1)}
    two = np.eye(2)
    centre = np.kron(two, np.kron(band[0], eye) + np.kron(eye, band[0]))
    ym, yp = (np.kron(two, np.kron(eye, band[s])) for s in (-1, 1))
    xm, xp = (np.kron(two, np.kron(band[s], eye)) for s in (-1, 1))
    zero = np.zeros_like(centre)
    own = np.block([[centre, ym], [yp, centre]])
    other = np.block([[zero, yp], [ym, zero]])
    left = np.block([[xm, zero], [zero, xm]])
    right = np.block([[xp, zero], [zero, xp]])
    return np.concatenate([own, other, left, right], axis=0).astype(np.float32)


def filter_kernel(
    counts, slot_id, owner, anchor, extent, coupling,
    x_ref, v_ref, p_ref, w_ref, o_ref,
    bufa, bufb, hi, lo, pm, pg, rows_ref, coef_ref, slot_d, slot_r,
):
    lane = lax.broadcasted_iota(jnp.int32, (8, 128), 1)
    sub = lax.broadcasted_iota(jnp.int32, (8, 128), 0)
    first_half = lane < 64
    upper = sub < 4
    reach = jnp.maximum(jnp.maximum((lane % 64) // 8, lane % 8), sub)
    me = counts[2]
    n_own, n_all = counts[0], counts[1]

    def prepare(slot, _):
        ident = slot_id[slot] - 1
        used = ident >= 0
        ident = jnp.maximum(ident, 0)
        rank = owner[ident]
        slab = rank % 8
        shift = lax.rem(slab - me + 12, 8) - 4
        slot_d[slot] = jnp.where(used, rank // 8, 0)
        slot_r[slot] = jnp.where(used, anchor[ident] + PAD + 128 * shift, PAD)
        keep = reach < jnp.where(used, extent[ident], 0)
        for p in range(2):
            value = jnp.where(keep, p_ref[ident, pl.ds(8 * p, 8), :], 0.0)
            gain = jnp.where(first_half, coupling[4 * ident + 2 * p], coupling[4 * ident + 2 * p + 1])
            pm[slot, pl.ds(8 * p, 8), :] = value
            pg[slot, pl.ds(8 * p, 8), :] = value * gain
        return 0

    lax.fori_loop(0, n_all, prepare, 0)

    row = lax.broadcasted_iota(jnp.int32, (128, 128), 0)
    col = lax.broadcasted_iota(jnp.int32, (128, 128), 1)
    ones = ((row < 64) == (col < 64)).astype(F32).astype(BF16)

    def apply(now, old, new, offset, base, rows, alpha, beta, count):
        def split(dx, _):
            for u in range(2):
                for h in range(2):
                    for r in range(0, rows, 16):
                        v = now[4 * dx + 2 * u + h, pl.ds(base + r, 16), :]
                        top = v.astype(BF16)
                        hi[u, dx, pl.ds(r, 16), pl.ds(128 * h, 128)] = top
                        lo[u, dx, pl.ds(r, 16), pl.ds(128 * h, 128)] = (v - top.astype(F32)).astype(BF16)
            return 0

        lax.fori_loop(0, 4, split, 0)

        def stencil(it, _):
            u, dx = it // 4, it % 4
            below, above = lax.rem(dx + 3, 4), lax.rem(dx + 1, 4)
            blocks = []
            for part in (hi, lo):
                for uu, xx in ((u, dx), (1 - u, dx), (u, below), (u, above)):
                    blocks.append(part[uu, xx, pl.ds(0, rows), :])
            acc = jnp.dot(jnp.concatenate(blocks, axis=1), w_ref[...], preferred_element_type=F32)
            for h in range(2):
                d = 4 * dx + 2 * u + h
                for r in range(0, rows, 8):
                    s = base + r
                    mid = now[d, pl.ds(s, 8), :]
                    val = acc[r : r + 8, 128 * h : 128 * h + 128] * (alpha * KIN / WSCALE)
                    val = val + (alpha * v_ref[d, pl.ds(s, 8), :]) * mid
                    for m in range(1, 7):
                        val = val + (alpha * KIN * STENCIL[m]) * (
                            now[d, pl.ds(s + m, 8), :] + now[d, pl.ds(s - m, 8), :]
                        )
                    if beta:
                        val = val - beta * old[d, pl.ds(s, 8), :]
                    new[d, pl.ds(s - offset, 8), :] = val
            return 0

        lax.fori_loop(0, 8, stencil, 0)

        def project(pair, _):
            prods = []
            for k in range(2):
                slot = 2 * pair + k
                box = now[slot_d[slot], pl.ds(slot_r[slot], 8), :]
                swapped = pltpu.roll(box, 64, 1)
                for p in range(2):
                    proj = pm[slot, pl.ds(8 * p, 8), :]
                    prods += [proj * box, proj * swapped]
            merged = []
            for i in range(4):
                a, b = prods[i], prods[i + 4]
                t = jnp.where(upper, a, b) + pltpu.roll(jnp.where(upper, b, a), 4, 0)
                t = t + pltpu.roll(t, 7, 0)
                merged.append(t + pltpu.roll(t, 6, 0))
            low = sub % 4
            out = merged[0]
            for i in range(1, 4):
                out = jnp.where(low == i, pltpu.roll(merged[i], i, 0), out)
            rows_ref[pl.ds(pl.multiple_of(8 * pair, 8), 8), :] = out
            return 0

        lax.fori_loop(0, count // 2, project, 0, unroll=False)

        def reduce(chunk, _):
            at = pl.multiple_of(32 * chunk, 32)
            v = rows_ref[pl.ds(at, 32), :]
            top = v.astype(BF16)
            rest = (v - top.astype(F32)).astype(BF16)
            both = jnp.dot(jnp.concatenate([top, rest], axis=0), ones, preferred_element_type=F32)
            coef_ref[pl.ds(at, 32), :] = alpha * (both[:32] + both[32:])
            return 0

        lax.fori_loop(0, count // 8, reduce, 0)

        def spread(slot, _):
            at = 4 * slot
            pieces = [
                jnp.broadcast_to(coef_ref[pl.ds(at + i, 1), :], (8, 128)) for i in range(4)
            ]
            p0, p1 = pg[slot, pl.ds(0, 8), :], pg[slot, pl.ds(8, 8), :]
            w = p0 * pieces[0] + p1 * pieces[2] + pltpu.roll(p0 * pieces[1] + p1 * pieces[3], 64, 1)
            d, r = slot_d[slot], slot_r[slot] - offset
            new[d, pl.ds(r, 8), :] = new[d, pl.ds(r, 8), :] + w
            return 0

        lax.fori_loop(0, count, spread, 0)

    plan = steps()
    chain = ((x_ref, None, bufb, 0, n_all), (bufb, x_ref, bufa, 0, n_all),
             (bufa, bufb, bufb, 0, n_all), (bufb, bufa, o_ref, PAD, n_own))
    for (now, old, new, offset, count), (base, rows), (alpha, beta) in zip(chain, RANGES, plan):
        apply(now, old, new, offset, base, rows, alpha, beta, count)


def run_filter(counts, slot_id, owner, anchor, extent, coupling, x, v, p, w):
    smem = pl.BlockSpec(memory_space=pltpu.SMEM)
    vmem = pl.BlockSpec(memory_space=pltpu.VMEM)
    return pl.pallas_call(
        filter_kernel,
        out_shape=jax.ShapeDtypeStruct((G, 128, 128), F32),
        in_specs=[smem] * 6 + [vmem] * 4,
        out_specs=vmem,
        scratch_shapes=[
            pltpu.VMEM((G, ROWS, 128), F32),
            pltpu.VMEM((G, ROWS, 128), F32),
            pltpu.VMEM((2, 4, RANGES[0][1], 256), BF16),
            pltpu.VMEM((2, 4, RANGES[0][1], 256), BF16),
            pltpu.VMEM((SLOTS, 16, 128), F32),
            pltpu.VMEM((SLOTS, 16, 128), F32),
            pltpu.VMEM((4 * SLOTS, 128), F32),
            pltpu.VMEM((4 * SLOTS, 128), F32),
            pltpu.SMEM((SLOTS,), jnp.int32),
            pltpu.SMEM((SLOTS,), jnp.int32),
        ],
        compiler_params=pltpu.CompilerParams(vmem_limit_bytes=56 * 2**20),
        name="chebyshev",
    )(counts, slot_id, owner, anchor, extent, coupling, x, v, p, w)


def slots(owner, anchor_z, me):
    slab = owner % 8
    own = slab == me
    before = (slab == (me + 7) % 8) & (anchor_z + MARGIN >= 128)
    after = (slab == (me + 1) % 8) & (anchor_z + B <= MARGIN)
    near = before | after
    ids = jnp.arange(owner.shape[0], dtype=jnp.int32)
    earlier = ids[None, :] < ids[:, None]
    n_own = jnp.sum(own.astype(jnp.int32))
    first = (n_own + 7) // 8 * 8
    n_all = first + (jnp.sum(near.astype(jnp.int32)) + 7) // 8 * 8
    at_own = jnp.sum((earlier & own[None, :]).astype(jnp.int32), axis=1)
    at_near = jnp.sum((earlier & near[None, :]).astype(jnp.int32), axis=1) + first
    at = jnp.where(own, at_own, jnp.where(near, at_near, -1))
    table = jnp.sum(
        jnp.where(at[None, :] == jnp.arange(SLOTS, dtype=jnp.int32)[:, None], ids[None, :] + 1, 0), axis=1
    )
    return jnp.stack([first, n_all, me]), table


def body(orbitals, potential, projectors, owner_rank, box_anchor, box_extent, coupling):
    plane = ("gx", "gy")
    me = lax.axis_index("gz")
    states = orbitals.shape[0]
    sent = jnp.swapaxes(orbitals.reshape(G, 128, 128), 1, 2)
    x = lax.all_to_all(sent, plane, 0, 0, tiled=True)
    v = jnp.swapaxes(potential.reshape(1, 64, 128), 1, 2) + DIAG
    v = lax.all_gather(v, plane, axis=0, tiled=True)
    p = projectors.reshape(8, 2, 2, 64, 8).transpose(0, 1, 4, 2, 3).reshape(8, 16, 128)
    p = lax.all_gather(p, ("gx", "gy", "gz"), axis=0, tiled=True)

    def extend(a):
        n = lax.axis_size("gz")
        up = lax.ppermute(a[:, 128 - HALO :], "gz", [(i, (i + 1) % n) for i in range(n)])
        down = lax.ppermute(a[:, :HALO], "gz", [((i + 1) % n, i) for i in range(n)])
        edge = jnp.zeros((G, PAD - HALO, a.shape[2]), F32)
        return jnp.concatenate([edge, up, a, down, edge], axis=1)

    x = extend(x)
    v = extend(v)
    v = jnp.concatenate([v, v], axis=2)
    counts, table = slots(owner_rank, box_anchor[2], me)
    w = weights()
    w = jnp.asarray(np.concatenate([w, w], axis=0)).astype(BF16)
    y = run_filter(
        counts, table, owner_rank, box_anchor[2], box_extent, coupling.reshape(-1), x, v, p, w
    )
    back = lax.all_to_all(y, plane, 0, 0, tiled=True)
    filtered = jnp.swapaxes(back, 1, 2).reshape(states, 8, 8, 128)
    flat = filtered.reshape(states, -1)
    part = jnp.dot(flat, flat.T, precision=lax.Precision.HIGHEST)
    total = lax.psum(part, ("gx", "gy", "gz")) / (32 * 32 * 1024)
    return filtered, total


def solution(mesh):
    return jax.shard_map(
        body,
        mesh=mesh,
        in_specs=(
            P(None, "gx", "gy", "gz"),
            P("gx", "gy", "gz"),
            P(("gx", "gy", "gz"), None, None),
            P(),
            P(),
            P(),
            P(),
        ),
        out_specs=(P(None, "gx", "gy", "gz"), P()),
        check_vma=False,
    )
```

time: 1530 us -> 313 us (0.20); the launches traced: 1500 us -> 310 us
  local copies, waits for them, and re-layouts: 626 us -> 16.2 us
  matrix products: 260 us -> 0.96 us
  loops' own time: 250 us -> 0 us
  waiting for transfers between devices: 142 us -> 21.9 us
  Pallas kernels: 0 us -> 117 us
  other arithmetic: 117 us -> 7.15 us
  blocking collectives: 65.2 us -> 114 us
    dot_general x194 -> x1, matrix products: 260 us -> 0.96 us  [body(): part = jnp.dot(flat, flat.T, precision=lax.Precision.HIGHEST)]
    another operation x4 -> x0, loops' own time: 250 us -> none  [nonlocal_term(): return lax.fori_loop(0, count, add_slot, jnp.zeros_like(field))]
    dynamic_update_slice x96 -> x0, local copies, waits for them, and re-layouts: 182 us -> none  [add_slot(): lax.dynamic_update_slice(nonlocal_sum, current + addition, start_cell)]
    slice x117 -> x3, local copies, waits for them, and re-layouts: 169 us -> 1.59 us  [the longest x2 0.86 us: extend(): down = lax.ppermute(a[:, :HALO], 'gz', [((i + 1) % n, i) for i in range(n)])]
    ppermute x24 -> x4, waiting for transfers between devices: 142 us -> 1.51 us  [the longest x2 1.5 us: extend(): down = lax.ppermute(a[:, :HALO], 'gz', [((i + 1) % n, i) for i in range(n)])]
    pallas_call x0 -> x1, Pallas kernels: none -> 117 us  [run_filter(): pl.pallas_call(filter_kernel, out_shape=jax.ShapeDtypeStruct((G, 128, 128...]
    dynamic_slice x96 -> x0, local copies, waits for them, and re-layouts: 105 us -> none  [add_slot(): lax.dynamic_slice(field, start_cell, (states, B, B, B))]
    dot_general x192 -> x0, local copies, waits for them, and re-layouts: 78.2 us -> none  [add_slot(): jnp.dot(coeffs, proj_box, precision=lax.Precision.HIGHEST)]
  transfers between devices with their start and end apart: 25 -> 6, of which waited for: 16 -> 3; matrix products, arithmetic and copies ran while one was open for 43% -> 6% of each run, Pallas kernels for 0% -> 0%
where the time goes in v1:
time: 313 us; the launch traced here: 310 us
  Pallas kernels  117 us (37%)
  blocking collectives  114 us (36%)
  waiting for transfers between devices  21.9 us (7%)
  starting transfers between devices  16.4 us (5%)
  local copies, waits for them, and re-layouts  16.2 us (5%)
  between operations  15.4 us (5%)
  other arithmetic  7.15 us (2%)
    pallas_call x1, Pallas kernels, run_filter(): pl.pallas_call(filter_kernel, out_shape=jax.ShapeDtypeStruct((G, 128, 128...  117 us
    psum x1, blocking collectives, body(): total = lax.psum(part, ('gx', 'gy', 'gz')) / (32 * 32 * 1024)  72.6 us
    all_gather x1, blocking collectives, body(): v = lax.all_gather(v, plane, axis=0, tiled=True)  21.6 us
    all_to_all x1, blocking collectives, body(): back = lax.all_to_all(y, plane, 0, 0, tiled=True)  20.2 us
    all_gather x1, waiting for transfers between devices, body(): p = lax.all_gather(p, ('gx', 'gy', 'gz'), axis=0, tiled=True)  14.6 us
    ppermute x2, starting transfers between devices, extend(): lax.ppermute(a[:, 128 - HALO:], 'gz', [(i, (i + 1) % n) for i in range(n)])  11.6 us
    unnamed x22, local copies, waits for them, and re-layouts  8.62 us
  transfers between devices with their start and end apart: 6, of which 3 were waited for; matrix products, arithmetic and copies ran while one was open for 6% of the time, Pallas kernels for 0%

profile of v1, /device:TPU:1, one launch (start us, length us, event | category | flops | bytes accessed | tf_op | source)
XLA Modules:
  0.0 309.6 jit_solution(4833362859859332696)
XLA Ops:
  7.2 0.9 copy.41
  9.0 0.8 reshape.33
  9.8 21.6 %all_gather.6 = f32[16,128,64]{1,2,0:T(8,128)S(1)} all-gather(f32[1,128,64]{1,2,0:T(8,128)S(1)} %add_bitcast_fusion), channel_id=1, replica_groups=mesh['gx'=4,'gy'=4,'gz'=8] {'gx','gy'}, dimensions={0}, use_global_device_ids=true | all-gather | bytes 557056 | tf_op jit(solution)/shard_map/all_gather | solution.py:257
  31.8 0.8 fusion.7
  32.6 6.8 %collective-permute-start.2 = (f32[16,32,64]{2,1,0:T(8,128)}, f32[16,32,64]{2,1,0:T(8,128)}, u32[]{:S(2)}, u32[]{:S(2)}) collective-permute-start(f32[16,32,64]{2,1,0:T(8,128)} %get-tuple-element.7), channel_id=1, source_target_pairs={{0,1},{1,2},{2,3},{3,4},{4,5},{5,6},{6,7},{7,0},{8,9},{9,10},{10,1... | collective-permute-start | bytes 393224 | tf_op jit(solution)/shard_map/ppermute | solution.py:263
  39.4 1.3 copy.37
  40.7 4.7 %all-to-all-start = ((f32[16,128,128]{2,1,0:T(8,128)}), f32[16,128,128]{2,1,0:T(8,128)S(1)}, u32[]{:S(2)}, u32[]{:S(2)}) async-start(f32[16,128,128]{2,1,0:T(8,128)} %bitcast.5), calls=%async_computation | async-start | bytes 2097152 | tf_op jit(solution)/shard_map/all_to_all | solution.py:255
  49.1 1.1 select_reduce_fusion.slot_id
  51.0 0.9 reshape.30.coupling
  52.6 1.7 constant_dynamic-update-slice_fusion.5
  54.3 1.1 constant_dynamic-update-slice_fusion.4
  55.4 0.7 constant_dynamic-update-slice_fusion.3
  56.1 5.7 %all-to-all-done = f32[16,128,128]{2,1,0:T(8,128)S(1)} async-done(((f32[16,128,128]{2,1,0:T(8,128)}), f32[16,128,128]{2,1,0:T(8,128)S(1)}, u32[]{:S(2)}, u32[]{:S(2)}) %all-to-all-start) | async-done | bytes 1048608 | tf_op jit(solution)/shard_map/all_to_all | solution.py:255
  61.9 4.9 %collective-permute-start = (f32[16,32,128]{2,1,0:T(8,128)S(1)}, f32[16,32,128]{2,1,0:T(8,128)S(1)}, u32[]{:S(2)}, u32[]{:S(2)}) collective-permute-start(f32[16,32,128]{2,1,0:T(8,128)S(1)} %get-tuple-element.9), channel_id=1, source_target_pairs={{0,1},{1,2},{2,3},{3,4},{4,5},{5,6},{6,7},{7,0},{8,9},{9,10},{10,1... | collective-permute-start | bytes 786440 | tf_op jit(solution)/shard_map/ppermute | solution.py:263
  67.4 3.8 %pad_maximum_fusion.v_ref = f32[16,208,128]{2,1,0:T(8,128)} fusion(f32[16,208,64]{2,1,0:T(8,128)} %broadcast_dynamic-update-slice_fusion.1), kind=kLoop, calls=%fused_computation.7 | loop fusion | flops 425984 | bytes 2555904 | tf_op jit(solution)/shard_map/concatenate | solution.py:270
  71.2 0.7 constant_dynamic-update-slice_fusion.2
  71.9 1.2 constant_dynamic-update-slice_fusion.1
  73.1 1.5 collective-permute-done.1
  74.6 0.7 constant_dynamic-update-slice_fusion
  76.0 14.6 %all-gather.2.cloned.1.call-done.p_ref = f32[1024,16,128]{2,1,0:T(8,128)} async-done(((f32[8,16,128]{2,1,0:T(8,128)}), f32[1024,16,128]{2,1,0:T(8,128)}) %all-gather.2.cloned.1.call-update) | async-done | bytes 8388624 | tf_op jit(solution)/shard_map/all_gather | solution.py:259
  90.6 117.2 %chebyshev.1 = f32[16,128,128]{2,1,0:T(8,128)} custom-call(s32[3]{0:T(128)} %pad_add_fusion.counts, s32[1040]{0:T(1024)} %select_reduce_fusion.slot_id, s32[1024]{0:T(1024)} %owner.1, s32[1024]{0:T(1024)} %bitcast.22, s32[1024]{0:T(1024)} %extent.1, f32[4096]{0:T(1024)} %reshape.30.coupling, f32[16,208,128]{2,1,0:T(8,128)} %broadcast_dynamic-update-slice_fusion.3.x_ref, ...), custom_call_target="tpu_custom_call" | custom-call | tf_op jit(solution)/shard_map/chebyshev/pallas_call | solution.py:208
  207.8 20.2 %all_to_all.10 = f32[16,128,128]{2,1,0:T(8,128)S(1)} all-to-all(f32[16,128,128]{2,1,0:T(8,128)} %chebyshev.1), channel_id=1, replica_groups=mesh['gx'=4,'gy'=4,'gz'=8] {'gx','gy'}, dimensions={0} | all-to-all | bytes 2097152 | tf_op jit(solution)/shard_map/all_to_all | solution.py:277
  228.6 1.0 fusion.9
  229.5 72.6 %psum.7 = f32[32,32]{1,0:T(8,128)S(1)} all-reduce(f32[32,32]{1,0:T(8,128)S(1)} %fusion.9), channel_id=1, replica_groups=mesh['gx'=4,'gy'=4,'gz'=8] {'gx','gy','gz'}, use_global_device_ids=true, to_apply=%region_5.6 | all-reduce | flops 1024 | bytes 8192 | tf_op jit(solution)/shard_map/psum | solution.py:281
  (38 shorter events, 7.7 us)
Async XLA Ops:
  7.2 2.6 copy-start.3
  7.2 83.5 %all-gather.2.cloned.1.call-start = ((), (), s32[]{:S(2)}) async-start(), calls=%async_computation.2 | async-start | bytes 8454144 | tf_op jit(solution)/shard_map/all_gather | solution.py:259
  9.8 29.6 %copy-start.1 = (f32[32,8,8,128]{3,2,1,0:T(8,128)S(1)}, f32[32,8,8,128]{3,2,1,0:T(8,128)}, u32[]{:S(2)}) copy-start(f32[32,8,8,128]{3,2,1,0:T(8,128)} %param.8) | copy-start | bytes 3145732
  32.6 20.0 %collective-permute-start.2 = (f32[16,32,64]{2,1,0:T(8,128)}, f32[16,32,64]{2,1,0:T(8,128)}, u32[]{:S(2)}, u32[]{:S(2)}) collective-permute-start(f32[16,32,64]{2,1,0:T(8,128)} %get-tuple-element.7), channel_id=1, source_target_pairs={{0,1},{1,2},{2,3},{3,4},{4,5},{5,6},{6,7},{7,0},{8,9},{9,10},{10,1... | collective-permute-start | bytes 393224 | tf_op jit(solution)/shard_map/ppermute | solution.py:263
  39.3 16.1 %collective-permute-start.3 = (f32[16,32,64]{2,1,0:T(8,128)}, f32[16,32,64]{2,1,0:T(8,128)S(1)}, u32[]{:S(2)}, u32[]{:S(2)}) collective-permute-start(f32[16,32,64]{2,1,0:T(8,128)} %get-tuple-element.6), channel_id=1, source_target_pairs={{1,0},{2,1},{3,2},{4,3},{5,4},{6,5},{7,6},{0,7},{9,8},{10,9},{11,1... | collective-permute-start | bytes 393224 | tf_op jit(solution)/shard_map/ppermute | solution.py:264
  39.3 6.8 %copy-start.4 = (s32[1024]{0:T(1024)S(1)}, s32[1024]{0:T(1024)}, u32[]{:S(2)}) copy-start(s32[1024]{0:T(1024)} %owner.1) | copy-start | bytes 12292
  40.7 10.1 %copy-start.5 = (f32[1024,4]{0,1:T(4,128)S(1)}, f32[1024,4]{0,1:T(4,128)}, u32[]{:S(2)}) copy-start(f32[1024,4]{0,1:T(4,128)} %param.14) | copy-start | bytes 49156
  40.7 21.2 %all-to-all-start = ((f32[16,128,128]{2,1,0:T(8,128)}), f32[16,128,128]{2,1,0:T(8,128)S(1)}, u32[]{:S(2)}, u32[]{:S(2)}) async-start(f32[16,128,128]{2,1,0:T(8,128)} %bitcast.5), calls=%async_computation | async-start | bytes 2097152 | tf_op jit(solution)/shard_map/all_to_all | solution.py:255
  46.1 9.3 %copy-start.2 = (s32[1,1024]{1,0:T(1,128)}, s32[1,1024]{1,0:T(1,128)S(1)}, u32[]{:S(2)}) copy-start(s32[1,1024]{1,0:T(1,128)S(1)} %slice.16) | copy-start | bytes 12292
  61.9 9.3 %collective-permute-start = (f32[16,32,128]{2,1,0:T(8,128)S(1)}, f32[16,32,128]{2,1,0:T(8,128)S(1)}, u32[]{:S(2)}, u32[]{:S(2)}) collective-permute-start(f32[16,32,128]{2,1,0:T(8,128)S(1)} %get-tuple-element.9), channel_id=1, source_target_pairs={{0,1},{1,2},{2,3},{3,4},{4,5},{5,6},{6,7},{7,0},{8,9},{9,10},{10,1... | collective-permute-start | bytes 786440 | tf_op jit(solution)/shard_map/ppermute | solution.py:263
  67.4 7.2 %collective-permute-start.1 = (f32[16,32,128]{2,1,0:T(8,128)S(1)}, f32[16,32,128]{2,1,0:T(8,128)S(1)}, u32[]{:S(2)}, u32[]{:S(2)}) collective-permute-start(f32[16,32,128]{2,1,0:T(8,128)S(1)} %get-tuple-element.8), channel_id=1, source_target_pairs={{1,0},{2,1},{3,2},{4,3},{5,4},{6,5},{7,6},{0,7},{9,8},{10,9},{11,1... | collective-permute-start | bytes 786440 | tf_op jit(solution)/shard_map/ppermute | solution.py:264
  228.3 1.2 copy-start
Sparse Core Ops, SparseCore 0:
  11.0 79.6 all-gather.1

commit v2 on v1

--- a/solution.py
+++ b/solution.py
@@ -35,7 +35,8 @@
 WSCALE = 35.0 / 32.0
 KIN = -0.5 / (SPACING * SPACING)
 DIAG = KIN * 3.0 * STENCIL[0] - MIDDLE
-SLOTS = 1040
+SLOTS = 1088
+CHUNK = 256
 F32 = jnp.float32
 BF16 = jnp.bfloat16
 
@@ -74,8 +75,8 @@
 
 def filter_kernel(
     counts, slot_id, owner, anchor, extent, coupling,
-    x_ref, v_ref, p_ref, w_ref, o_ref,
-    bufa, bufb, hi, lo, pm, pg, rows_ref, coef_ref, slot_d, slot_r,
+    x_ref, vp_ref, p_ref, w_ref, o_ref,
+    v_ref, bufa, bufb, hi, lo, pm, pg, rows_ref, coef_ref, slot_d, slot_r,
 ):
     lane = lax.broadcasted_iota(jnp.int32, (8, 128), 1)
     sub = lax.broadcasted_iota(jnp.int32, (8, 128), 0)
@@ -103,6 +104,16 @@
         return 0
 
     lax.fori_loop(0, n_all, prepare, 0)
+
+    def unpack(d, _):
+        for r in range(0, 96, 8):
+            pair = vp_ref[d, pl.ds(r, 8), :]
+            swapped = pltpu.roll(pair, 64, 1)
+            v_ref[d, pl.ds(8 + 2 * r, 8, stride=2), :] = jnp.where(first_half, pair, swapped) + DIAG
+            v_ref[d, pl.ds(9 + 2 * r, 8, stride=2), :] = jnp.where(first_half, swapped, pair) + DIAG
+        return 0
+
+    lax.fori_loop(0, G, unpack, 0)
 
     row = lax.broadcasted_iota(jnp.int32, (128, 128), 0)
     col = lax.broadcasted_iota(jnp.int32, (128, 128), 1)
@@ -147,53 +158,59 @@
 
         lax.fori_loop(0, 8, stencil, 0)
 
-        def project(pair, _):
-            prods = []
-            for k in range(2):
-                slot = 2 * pair + k
-                box = now[slot_d[slot], pl.ds(slot_r[slot], 8), :]
-                swapped = pltpu.roll(box, 64, 1)
-                for p in range(2):
-                    proj = pm[slot, pl.ds(8 * p, 8), :]
-                    prods += [proj * box, proj * swapped]
-            merged = []
-            for i in range(4):
-                a, b = prods[i], prods[i + 4]
-                t = jnp.where(upper, a, b) + pltpu.roll(jnp.where(upper, b, a), 4, 0)
-                t = t + pltpu.roll(t, 7, 0)
-                merged.append(t + pltpu.roll(t, 6, 0))
-            low = sub % 4
-            out = merged[0]
-            for i in range(1, 4):
-                out = jnp.where(low == i, pltpu.roll(merged[i], i, 0), out)
-            rows_ref[pl.ds(pl.multiple_of(8 * pair, 8), 8), :] = out
+        low = sub % 4
+
+        def project(group, _):
+            for q in range(4):
+                prods = []
+                for k in range(2):
+                    slot = 8 * group + 2 * q + k
+                    box = now[slot_d[slot], pl.ds(slot_r[slot], 8), :]
+                    swapped = pltpu.roll(box, 64, 1)
+                    for p in range(2):
+                        proj = pm[slot, pl.ds(8 * p, 8), :]
+                        prods += [proj * box, proj * swapped]
+                out = None
+                for i in range(4):
+                    a, b = prods[i], prods[i + 4]
+                    t = jnp.where(upper, a, b) + pltpu.roll(jnp.where(upper, b, a), 4, 0)
+                    t = t + pltpu.roll(t, 7, 0)
+                    t = t + pltpu.roll(t, 6, 0)
+                    out = t if i == 0 else jnp.where(low == i, pltpu.roll(t, i, 0), out)
+                rows_ref[pl.ds(pl.multiple_of(32 * group, 32) + 8 * q, 8), :] = out
             return 0
 
-        lax.fori_loop(0, count // 2, project, 0, unroll=False)
+        lax.fori_loop(0, count // 8, project, 0)
 
         def reduce(chunk, _):
-            at = pl.multiple_of(32 * chunk, 32)
-            v = rows_ref[pl.ds(at, 32), :]
+            at = pl.multiple_of(CHUNK * chunk, CHUNK)
+            v = rows_ref[pl.ds(at, CHUNK), :]
             top = v.astype(BF16)
             rest = (v - top.astype(F32)).astype(BF16)
             both = jnp.dot(jnp.concatenate([top, rest], axis=0), ones, preferred_element_type=F32)
-            coef_ref[pl.ds(at, 32), :] = alpha * (both[:32] + both[32:])
+            coef_ref[pl.ds(at, CHUNK), :] = alpha * (both[:CHUNK] + both[CHUNK:])
             return 0
 
-        lax.fori_loop(0, count // 8, reduce, 0)
-
-        def spread(slot, _):
-            at = 4 * slot
-            pieces = [
-                jnp.broadcast_to(coef_ref[pl.ds(at + i, 1), :], (8, 128)) for i in range(4)
-            ]
-            p0, p1 = pg[slot, pl.ds(0, 8), :], pg[slot, pl.ds(8, 8), :]
-            w = p0 * pieces[0] + p1 * pieces[2] + pltpu.roll(p0 * pieces[1] + p1 * pieces[3], 64, 1)
-            d, r = slot_d[slot], slot_r[slot] - offset
-            new[d, pl.ds(r, 8), :] = new[d, pl.ds(r, 8), :] + w
+        lax.fori_loop(0, (4 * count + CHUNK - 1) // CHUNK, reduce, 0)
+
+        def spread(group, _):
+            adds = []
+            for q in range(8):
+                slot = 8 * group + q
+                at = 4 * slot
+                pieces = [
+                    jnp.broadcast_to(coef_ref[pl.ds(at + i, 1), :], (8, 128)) for i in range(4)
+                ]
+                p0, p1 = pg[slot, pl.ds(0, 8), :], pg[slot, pl.ds(8, 8), :]
+                w = p0 * pieces[0] + p1 * pieces[2]
+                adds.append(w + pltpu.roll(p0 * pieces[1] + p1 * pieces[3], 64, 1))
+            for q in range(8):
+                slot = 8 * group + q
+                d, r = slot_d[slot], slot_r[slot] - offset
+                new[d, pl.ds(r, 8), :] = new[d, pl.ds(r, 8), :] + adds[q]
             return 0
 
-        lax.fori_loop(0, count, spread, 0)
+        lax.fori_loop(0, count // 8, spread, 0)
 
     plan = steps()
     chain = ((x_ref, None, bufb, 0, n_all), (bufb, x_ref, bufa, 0, n_all),
@@ -211,6 +228,7 @@
         in_specs=[smem] * 6 + [vmem] * 4,
         out_specs=vmem,
         scratch_shapes=[
+            pltpu.VMEM((G, ROWS, 128), F32),
             pltpu.VMEM((G, ROWS, 128), F32),
             pltpu.VMEM((G, ROWS, 128), F32),
             pltpu.VMEM((2, 4, RANGES[0][1], 256), BF16),
@@ -225,6 +243,309 @@
         compiler_params=pltpu.CompilerParams(vmem_limit_bytes=56 * 2**20),
         name="chebyshev",
     )(counts, slot_id, owner, anchor, extent, coupling, x, v, p, w)
+
+
+MESH = pl.DeviceIdType.MESH
+PARTS = ((0, 48, 24, (0, 1, 2)), (48, 40, 24, (1, 2, 0)), (88, 40, 24, (2, 0, 1)))
+V_PARTS = ((0, 32, 16, (0, 1)), (32, 32, 16, (1, 0)))
+
+
+def position():
+    return lax.axis_index("gx"), lax.axis_index("gy"), lax.axis_index("gz")
+
+
+def plane_peer(offset):
+    gx, gy, gz = position()
+    return (lax.rem(gx + offset // 4, 4), lax.rem(gy + offset % 4, 4), gz)
+
+
+def plane_source(offset):
+    gx, gy, _ = position()
+    return 4 * lax.rem(gx + 4 - offset // 4, 4) + lax.rem(gy + 4 - offset % 4, 4)
+
+
+def line_peer(offset):
+    gx, gy, gz = position()
+    return (gx, gy, lax.rem(gz + offset, 8))
+
+
+def greet():
+    sem = pltpu.get_barrier_semaphore()
+
+    def plane(o, _):
+        pl.semaphore_signal(sem, inc=1, device_id=plane_peer(o), device_id_type=MESH)
+        return 0
+
+    def line(o, _):
+        pl.semaphore_signal(sem, inc=1, device_id=line_peer(o), device_id_type=MESH)
+        return 0
+
+    lax.fori_loop(1, 16, plane, 0)
+    lax.fori_loop(1, 8, line, 0)
+    pl.semaphore_wait(sem, 22)
+
+
+def remote(src, dst, send, recv, target):
+    return pltpu.make_async_remote_copy(
+        src_ref=src, dst_ref=dst, send_sem=send, recv_sem=recv, device_id=target, device_id_type=MESH
+    )
+
+
+def gather_kernel(
+    sent, vown, pown, x_out, v_out, p_out,
+    a2a_send, a2a_recv, p_send, p_recv, v_send, v_recv, twin_send, twin_recv, halo_send, halo_recv, here,
+):
+    gx, gy, gz = position()
+    y, core = gz // 2, gz % 2
+    mine = 4 * gx + gy
+    local = [
+        pltpu.make_async_copy(pown, p_out.at[gx, gy, y, core], here.at[0]),
+        pltpu.make_async_copy(vown, v_out.at[gx, gy, pl.ds(16, 64)], here.at[1]),
+        pltpu.make_async_copy(sent.at[mine], x_out.at[mine, pl.ds(PAD, 128)], here.at[2]),
+    ]
+    for copy in local:
+        copy.start()
+    greet()
+    where = (gx, gy, y)
+    sizes = (4, 4, 4)
+
+    def neighbour(dim, step):
+        at = list(where)
+        at[dim] = lax.rem(at[dim] + step + 4, 4)
+        return (at[0], at[1], 2 * at[2] + core)
+
+    def p_view(held, dim, at, start, rows):
+        idx = [pl.ds(0, 4) if k in held else where[k] for k in range(3)]
+        if dim is not None:
+            idx[dim] = at
+        return p_out.at[idx[0], idx[1], idx[2], core, pl.ds(start, rows)]
+
+    def v_view(held, dim, at, start, rows):
+        idx = [pl.ds(0, 4) if k in held else where[k] for k in range(2)]
+        if dim is not None:
+            idx[dim] = at
+        return v_out.at[idx[0], idx[1], pl.ds(16 + start, rows)]
+
+    def phase_copies(view, part, phase, send, recv):
+        start, rows, half, order = part
+        dim, held = order[phase], order[:phase]
+        me = where[dim]
+        below, above = lax.rem(me + 3, 4), lax.rem(me + 1, 4)
+        base = 4 * phase
+
+        def make(k, src, target):
+            return remote(src, src, send.at[base + k], recv.at[base + k], target)
+
+        own = view(held, dim, me, start, rows)
+        first = [make(0, own, neighbour(dim, 1)), make(1, own, neighbour(dim, -1))]
+        second = [
+            make(2, view(held, dim, below, start, half), neighbour(dim, 1)),
+            make(3, view(held, dim, above, start + half, rows - half), neighbour(dim, -1)),
+        ]
+        return first, second
+
+    def a2a(o):
+        peer = plane_peer(o)
+        target = 4 * peer[0] + peer[1]
+        return remote(
+            sent.at[target], x_out.at[mine, pl.ds(PAD, 128)], a2a_send.at[o], a2a_recv.at[o], peer
+        )
+
+    def send_a2a(lo_o, hi_o):
+        def step(o, _):
+            a2a(o).start()
+            return 0
+
+        lax.fori_loop(lo_o, hi_o, step, 0)
+
+    for copy in local:
+        copy.wait()
+    partner = (gx, gy, gz + 1 - 2 * core)
+
+    def twin(k, part, view_args):
+        src = p_view(*view_args)
+        return remote(src, src, twin_send.at[k, part], twin_recv.at[k, part], partner)
+
+    p_steps = [[phase_copies(p_view, part, ph, p_send.at[i], p_recv.at[i]) for ph in range(3)]
+               for i, part in enumerate(PARTS)]
+    v_steps = [[phase_copies(v_view, part, ph, v_send.at[i], v_recv.at[i]) for ph in range(2)]
+               for i, part in enumerate(V_PARTS)]
+    twins = []
+    cuts = [1, 4, 7, 10, 13, 16, 16]
+    for ph in range(3):
+        for st in range(2):
+            k = 2 * ph + st
+            group = [p_steps[i][ph][st] for i in range(3)]
+            if ph < 2:
+                group += [v_steps[i][ph][st] for i in range(2)]
+            for copies in group:
+                for copy in copies:
+                    copy.start()
+            if cuts[k] < cuts[k + 1]:
+                send_a2a(cuts[k], cuts[k + 1])
+            for copies in group:
+                for copy in copies:
+                    copy.wait()
+            new = []
+            for i, (start, rows, half, order) in enumerate(PARTS):
+                d3, held = order[2], order[:2]
+                me = where[d3]
+                if k == 3:
+                    new.append(twin(0, i, (held, d3, me, start, rows)))
+                if k == 4:
+                    new.append(twin(1, i, (held, d3, lax.rem(me + 1, 4), start, rows)))
+                    new.append(twin(2, i, (held, d3, lax.rem(me + 3, 4), start, rows)))
+                if k == 5:
+                    new.append(twin(3, i, (held, d3, lax.rem(me + 2, 4), start, rows)))
+            for copy in new:
+                copy.start()
+            twins += new
+
+    def finish_a2a(o, _):
+        a2a(o).wait()
+        return 0
+
+    lax.fori_loop(1, 16, finish_a2a, 0)
+    right, left = line_peer(1), line_peer(7)
+    whole = pl.ds(0, 4)
+    halos = [
+        remote(x_out.at[pl.ds(0, G), pl.ds(PAD + 128 - HALO, HALO)], x_out.at[pl.ds(0, G), pl.ds(PAD - HALO, HALO)],
+               halo_send.at[0], halo_recv.at[0], right),
+        remote(x_out.at[pl.ds(0, G), pl.ds(PAD, HALO)], x_out.at[pl.ds(0, G), pl.ds(PAD + 128, HALO)],
+               halo_send.at[1], halo_recv.at[1], left),
+        remote(v_out.at[whole, whole, pl.ds(64, 16)], v_out.at[whole, whole, pl.ds(0, 16)],
+               halo_send.at[2], halo_recv.at[2], right),
+        remote(v_out.at[whole, whole, pl.ds(16, 16)], v_out.at[whole, whole, pl.ds(80, 16)],
+               halo_send.at[3], halo_recv.at[3], left),
+    ]
+    for copy in halos:
+        copy.start()
+    for copy in halos + twins:
+        copy.wait()
+
+
+def run_gather(sent, vown, pown):
+    vmem = pl.BlockSpec(memory_space=pltpu.VMEM)
+    hbm = pl.BlockSpec(memory_space=pltpu.HBM)
+    dma = pltpu.SemaphoreType.DMA
+    return pl.pallas_call(
+        gather_kernel,
+        out_shape=(
+            jax.ShapeDtypeStruct((G, ROWS, 128), F32),
+            jax.ShapeDtypeStruct((4, 4, 96, 128), F32),
+            jax.ShapeDtypeStruct((4, 4, 4, 2, 128, 128), F32),
+        ),
+        in_specs=[vmem] * 3,
+        out_specs=(hbm, hbm, hbm),
+        scratch_shapes=[
+            dma((16,)), dma((16,)), dma((3, 12)), dma((3, 12)), dma((2, 8)), dma((2, 8)),
+            dma((4, 3)), dma((4, 3)), dma((4,)), dma((4,)), dma((3,)),
+        ],
+        compiler_params=pltpu.CompilerParams(collective_id=1, has_side_effects=True),
+        name="gather",
+    )(sent, vown, pown)
+
+
+def return_kernel(
+    y, out, total, recv, gram_a, gram_b, a2a_send, a2a_recv, a_send, a_recv, b_send, b_recv, here,
+):
+    gx, gy, gz = position()
+    mine = 4 * gx + gy
+    own = pltpu.make_async_copy(y.at[mine], recv.at[mine], here.at[0])
+    own.start()
+    greet()
+
+    def a2a(o):
+        peer = plane_peer(o)
+        return remote(
+            y.at[4 * peer[0] + peer[1]], recv.at[mine], a2a_send.at[o], a2a_recv.at[o], peer
+        )
+
+    def send(o, _):
+        a2a(o).start()
+        return 0
+
+    lax.fori_loop(1, 16, send, 0)
+
+    def place(source):
+        out[pl.ds(pl.multiple_of(128 * source, 128), 128), :] = recv[source].T
+
+    own.wait()
+    place(mine)
+
+    def receive(o, _):
+        a2a(o).wait()
+        place(plane_source(o))
+        return 0
+
+    lax.fori_loop(1, 16, receive, 0)
+
+    def gram(c, acc):
+        cells = jnp.concatenate([out[pl.ds(8 * c + i, 32, stride=64), :] for i in range(8)], axis=1)
+        top = cells.astype(BF16)
+        rest = (cells - top.astype(F32)).astype(BF16)
+        both = jnp.concatenate([top, rest], axis=0)
+        return acc + lax.dot_general(both, both, (((1,), (1,)), ((), ())), preferred_element_type=F32)
+
+    acc = lax.fori_loop(0, 8, gram, jnp.zeros((64, 64), F32))
+    g = acc[:32, :32] + (acc[:32, 32:] + acc[32:, :32])
+    gram_a[mine] = jnp.concatenate([g[8 * b : 8 * b + 8] for b in range(4)], axis=1)
+
+    def plane(o):
+        return remote(gram_a.at[mine], gram_a.at[mine], a_send.at[o], a_recv.at[o], plane_peer(o))
+
+    def line(o):
+        return remote(gram_b.at[gz], gram_b.at[gz], b_send.at[o], b_recv.at[o], line_peer(o))
+
+    def start_plane(o, _):
+        plane(o).start()
+        return 0
+
+    def wait_plane(o, _):
+        plane(o).wait()
+        return 0
+
+    def start_line(o, _):
+        line(o).start()
+        return 0
+
+    def wait_line(o, _):
+        line(o).wait()
+        return 0
+
+    lax.fori_loop(1, 16, start_plane, 0)
+    lax.fori_loop(1, 16, wait_plane, 0)
+    acc = gram_a[0]
+    for i in range(1, 16):
+        acc = acc + gram_a[i]
+    gram_b[gz] = acc
+    lax.fori_loop(1, 8, start_line, 0)
+    lax.fori_loop(1, 8, wait_line, 0)
+    acc = gram_b[0]
+    for i in range(1, 8):
+        acc = acc + gram_b[i]
+    acc = acc * (1.0 / (32 * 32 * 1024))
+    for b in range(4):
+        total[pl.ds(8 * b, 8), :] = acc[:, 32 * b : 32 * b + 32]
+
+
+def run_return(y):
+    vmem = pl.BlockSpec(memory_space=pltpu.VMEM)
+    dma = pltpu.SemaphoreType.DMA
+    return pl.pallas_call(
+        return_kernel,
+        out_shape=(jax.ShapeDtypeStruct((2048, 128), F32), jax.ShapeDtypeStruct((32, 32), F32)),
+        in_specs=[vmem],
+        out_specs=(vmem, vmem),
+        scratch_shapes=[
+            pltpu.VMEM((G, 128, 128), F32),
+            pltpu.VMEM((G, 8, 128), F32),
+            pltpu.VMEM((8, 8, 128), F32),
+            dma((16,)), dma((16,)), dma((16,)), dma((16,)), dma((8,)), dma((8,)), dma((1,)),
+        ],
+        compiler_params=pltpu.CompilerParams(collective_id=2, has_side_effects=True),
+        name="giveback",
+    )(y)
 
 
 def slots(owner, anchor_z, me):
@@ -248,38 +569,21 @@
 
 
 def body(orbitals, potential, projectors, owner_rank, box_anchor, box_extent, coupling):
-    plane = ("gx", "gy")
     me = lax.axis_index("gz")
     states = orbitals.shape[0]
     sent = jnp.swapaxes(orbitals.reshape(G, 128, 128), 1, 2)
-    x = lax.all_to_all(sent, plane, 0, 0, tiled=True)
-    v = jnp.swapaxes(potential.reshape(1, 64, 128), 1, 2) + DIAG
-    v = lax.all_gather(v, plane, axis=0, tiled=True)
-    p = projectors.reshape(8, 2, 2, 64, 8).transpose(0, 1, 4, 2, 3).reshape(8, 16, 128)
-    p = lax.all_gather(p, ("gx", "gy", "gz"), axis=0, tiled=True)
-
-    def extend(a):
-        n = lax.axis_size("gz")
-        up = lax.ppermute(a[:, 128 - HALO :], "gz", [(i, (i + 1) % n) for i in range(n)])
-        down = lax.ppermute(a[:, :HALO], "gz", [((i + 1) % n, i) for i in range(n)])
-        edge = jnp.zeros((G, PAD - HALO, a.shape[2]), F32)
-        return jnp.concatenate([edge, up, a, down, edge], axis=1)
-
-    x = extend(x)
-    v = extend(v)
-    v = jnp.concatenate([v, v], axis=2)
+    v = jnp.swapaxes(potential.reshape(64, 128), 0, 1).reshape(64, 128)
+    p = projectors.reshape(8, 2, 2, 64, 8).transpose(0, 1, 4, 2, 3).reshape(128, 128)
+    x, v, p = run_gather(sent, v, p)
     counts, table = slots(owner_rank, box_anchor[2], me)
     w = weights()
     w = jnp.asarray(np.concatenate([w, w], axis=0)).astype(BF16)
     y = run_filter(
-        counts, table, owner_rank, box_anchor[2], box_extent, coupling.reshape(-1), x, v, p, w
+        counts, table, owner_rank, box_anchor[2], box_extent, coupling.reshape(-1),
+        x, v.reshape(G, 96, 128), p.reshape(1024, 16, 128), w,
     )
-    back = lax.all_to_all(y, plane, 0, 0, tiled=True)
-    filtered = jnp.swapaxes(back, 1, 2).reshape(states, 8, 8, 128)
-    flat = filtered.reshape(states, -1)
-    part = jnp.dot(flat, flat.T, precision=lax.Precision.HIGHEST)
-    total = lax.psum(part, ("gx", "gy", "gz")) / (32 * 32 * 1024)
-    return filtered, total
+    filtered, total = run_return(y)
+    return filtered.reshape(states, 8, 8, 128), total
 
 
 def solution(mesh):

time: 313 us -> 159 us (0.51); the launches traced: 310 us -> 161 us
  blocking collectives: 114 us -> 0 us
  Pallas kernels: 117 us -> 144 us
  waiting for transfers between devices: 21.9 us -> 0 us
  starting transfers between devices: 16.4 us -> 0 us
  between operations: 15.4 us -> 2.14 us
  local copies, waits for them, and re-layouts: 16.2 us -> 11.3 us
  other arithmetic: 7.15 us -> 3.49 us
    pallas_call x0 -> x2, Pallas kernels: none -> 92.6 us  [the longest x1 60.9 us: run_gather(): pl.pallas_call(gather_kernel, out_shape=(jax.ShapeDtypeStruct((G, ROWS, 1...]
    psum x1 -> x0, blocking collectives: 72.6 us -> none  [body(): total = lax.psum(part, ('gx', 'gy', 'gz')) / (32 * 32 * 1024)]
    pallas_call x1, Pallas kernels: 117 us -> 51.6 us  [run_filter(): pl.pallas_call(filter_kernel, out_shape=jax.ShapeDtypeStruct((G, 128, 128...]
    all_gather x1 -> x0, blocking collectives: 21.6 us -> none  [body(): v = lax.all_gather(v, plane, axis=0, tiled=True)]
    all_to_all x1 -> x0, blocking collectives: 20.2 us -> none  [body(): back = lax.all_to_all(y, plane, 0, 0, tiled=True)]
    all_gather x1 -> x0, waiting for transfers between devices: 14.6 us -> none  [body(): p = lax.all_gather(p, ('gx', 'gy', 'gz'), axis=0, tiled=True)]
    ppermute x4 -> x0, starting transfers between devices: 11.6 us -> none  [the longest x2 11.6 us: extend(): lax.ppermute(a[:, 128 - HALO:], 'gz', [(i, (i + 1) % n) for i in range(n)])]
    all_to_all x1 -> x0, waiting for transfers between devices: 5.71 us -> none  [body(): x = lax.all_to_all(sent, plane, 0, 0, tiled=True)]
  transfers between devices with their start and end apart: 6 -> 0, of which waited for: 3 -> 0; matrix products, arithmetic and copies ran while one was open for 6% -> 0% of each run, Pallas kernels for 0% -> 0%
where the time goes in v2:
time: 159 us; the launch traced here: 161 us
  Pallas kernels  144 us (91%)
  local copies, waits for them, and re-layouts  11.3 us (7%)
  other arithmetic  3.49 us (2%)
  between operations  2.14 us (1%)
    pallas_call x1, Pallas kernels, run_gather(): pl.pallas_call(gather_kernel, out_shape=(jax.ShapeDtypeStruct((G, ROWS, 1...  60.9 us
    pallas_call x1, Pallas kernels, run_filter(): pl.pallas_call(filter_kernel, out_shape=jax.ShapeDtypeStruct((G, 128, 128...  51.6 us
    pallas_call x1, Pallas kernels, run_return(): pl.pallas_call(return_kernel, out_shape=(jax.ShapeDtypeStruct((2048, 128)...  31.8 us
    unnamed x10, local copies, waits for them, and re-layouts  4.72 us

profile of v2, /device:TPU:1, one launch (start us, length us, event | category | flops | bytes accessed | tf_op | source)
XLA Modules:
  0.0 161.1 jit_solution(13094899853620550488)
XLA Ops:
  0.6 0.0 copy-start.1
  0.6 0.0 copy-start.2
  0.7 0.7 slice.4
  1.4 1.4 convert_reduce_fusion.2
  2.8 0.4 convert_reduce_fusion
  3.9 1.1 select_reduce_fusion.slot_id
  5.7 0.6 pad_add_fusion.counts
  6.3 0.9 copy.20
  7.2 0.6 reshape.43
  7.8 0.3 copy.21
  8.1 0.8 reshape.44.pown
  8.8 2.5 %copy.18 = f32[16,128,128]{1,2,0:T(8,128)} copy(f32[16,128,128]{2,1,0:T(8,128)} %bitcast.17) | data formatting | bytes 2097152 | tf_op jit(solution)/shard_map/reshape | solution.py:574
  11.4 0.0 copy-done.1
  11.4 0.1 copy.19
  11.5 0.7 reshape.42.vown
  12.2 60.9 %gather.1 = (f32[16,208,128]{2,1,0:T(8,128)}, f32[4,4,96,128]{3,2,1,0:T(8,128)}, f32[4,4,4,2,128,128]{5,4,3,2,1,0:T(8,128)}) custom-call(f32[16,128,128]{2,1,0:T(8,128)} %bitcast.15, f32[64,128]{1,0:T(8,128)} %reshape.42.vown, f32[128,128]{1,0:T(8,128)} %reshape.44.pown), custom_call_target="tpu_custom_call" | custom-call | tf_op jit(solution)/shard_map/gather/pallas_call | solution.py:431
  73.0 0.0 copy-done.2
  73.1 0.2 copy.17
  73.3 0.9 reshape.39.coupling
  74.2 0.0 copy-done
  74.2 51.6 %chebyshev.1.y = f32[16,128,128]{2,1,0:T(8,128)} custom-call(s32[3]{0:T(128)} %pad_add_fusion.counts, s32[1088]{0:T(1024)} %select_reduce_fusion.slot_id, s32[1024]{0:T(1024)} %owner.1, s32[1024]{0:T(1024)} %bitcast.22, s32[1024]{0:T(1024)} %extent.1, f32[4096]{0:T(1024)} %reshape.39.coupling, f32[16,208,128]{2,1,0:T(8,128)} %get-tuple-element.7.x_ref, ...), custom_call_target="tpu_custom_call" | custom-call | tf_op jit(solution)/shard_map/chebyshev/pallas_call | solution.py:225
  125.7 31.8 %giveback.1 = (f32[2048,128]{1,0:T(8,128)}, f32[32,32]{1,0:T(8,128)}) custom-call(f32[16,128,128]{2,1,0:T(8,128)} %chebyshev.1.y), custom_call_target="tpu_custom_call" | custom-call | tf_op jit(solution)/shard_map/giveback/pallas_call | solution.py:535
  157.5 2.3 %copy.24 = f32[32,8,8,128]{3,2,1,0:T(8,128)} copy(f32[32,8,8,128]{3,2,1,0:T(8,128)} %bitcast.18) | data formatting | bytes 2097152
  159.8 1.3 copy.25
  (3 shorter events, 0.0 us)
Async XLA Ops:
  0.6 10.8 %copy-start.1 = (f32[8,8,128]{2,1,0:T(8,128)S(1)}, f32[8,8,128]{2,1,0:T(8,128)}, u32[]{:S(2)}) copy-start(f32[8,8,128]{2,1,0:T(8,128)} %param.9) | copy-start | bytes 98308
  0.6 72.4 %copy-start.2 = (f32[1024,4]{0,1:T(4,128)S(1)}, f32[1024,4]{0,1:T(4,128)}, u32[]{:S(2)}) copy-start(f32[1024,4]{0,1:T(4,128)} %param.14) | copy-start | bytes 49156
  1.4 72.8 %copy-start = (s32[1,1024]{1,0:T(1,128)}, s32[1,1024]{1,0:T(1,128)S(1)}, u32[]{:S(2)}) copy-start(s32[1,1024]{1,0:T(1,128)S(1)} %slice.4) | copy-start | bytes 12292

commit v3 on v2

v3 whole, which is shorter than its diff:
```python
import functools

import jax
import jax.numpy as jnp
import numpy as np
from jax import lax
from jax.experimental import pallas as pl
from jax.experimental.pallas import tpu as pltpu
from jax.sharding import PartitionSpec as P

B = 8
DEGREE = 4
STENCIL = (
    -5369.0 / 1800.0,
    12.0 / 7.0,
    -15.0 / 56.0,
    10.0 / 189.0,
    -1.0 / 112.0,
    2.0 / 1925.0,
    -1.0 / 16632.0,
)
SPACING = 0.5
LOW_EDGE = -2.5
CUTOFF = 4.0
UPPER = 60.0
HALF = (UPPER - CUTOFF) / 2.0
MIDDLE = (UPPER + CUTOFF) / 2.0

G = 16
PAD = 40
ROWS = 208
HALO = 32
MARGIN = 27
RANGES = ((16, 176), (24, 160), (32, 144), (40, 128))
WSCALE = 35.0 / 32.0
KIN = -0.5 / (SPACING * SPACING)
DIAG = KIN * 3.0 * STENCIL[0] - MIDDLE
SLOTS = 1040
F32 = jnp.float32
BF16 = jnp.bfloat16


def steps():
    sigma_one = HALF / (LOW_EDGE - MIDDLE)
    sigma = sigma_one
    out = [(sigma_one / HALF, 0.0)]
    for _ in range(1, DEGREE):
        nxt = 1.0 / (2.0 / sigma_one - sigma)
        out.append((2.0 * nxt / HALF, sigma * nxt))
        sigma = nxt
    return out


def weights():
    c = np.asarray(STENCIL, np.float64) * WSCALE

    def coef(m):
        m = abs(m)
        return c[m] if 1 <= m <= 6 else 0.0

    eye = np.eye(8)
    band = {s: np.array([[coef(8 * s + a - b) for b in range(8)] for a in range(8)]) for s in (-1, 0, 1)}
    two = np.eye(2)
    centre = np.kron(two, np.kron(band[0], eye) + np.kron(eye, band[0]))
    ym, yp = (np.kron(two, np.kron(eye, band[s])) for s in (-1, 1))
    xm, xp = (np.kron(two, np.kron(band[s], eye)) for s in (-1, 1))
    zero = np.zeros_like(centre)
    own = np.block([[centre, zero], [zero, centre]])
    across_x = np.block([[xp, xm], [xm, xp]])
    across_y = np.block([[yp, ym], [ym, yp]])
    both = [np.concatenate([own, across_x]), across_y]
    return np.concatenate([both[0], both[0], both[1], both[1]], axis=0).astype(np.float32)


def filter_kernel(
    table, owner, anchor, extent, coupling,
    x_ref, vp_ref, p_hbm, w_ref, o_ref,
    p_ref, v_ref, bufa, bufb, hi, lo, pm, gains, prods, slot_d, slot_r, load_sem,
):
    lane = lax.broadcasted_iota(jnp.int32, (8, 128), 1)
    sub = lax.broadcasted_iota(jnp.int32, (8, 128), 0)
    first_half = lane < 64
    upper = sub < 4
    low = sub % 4
    reach = jnp.maximum(jnp.maximum((lane % 64) // 8, lane % 8), sub)
    me = lax.axis_index("gz")
    n_own, n_all = table[15, 0], table[15, 1]

    load = pltpu.make_async_copy(p_hbm, p_ref, load_sem)
    load.start()

    def prepare(group, _):
        for q in range(8):
            slot = 8 * group + q
            ident = table[slot // 128, slot % 128] - 1
            used = ident >= 0
            ident = jnp.maximum(ident, 0)
            rank = owner[ident]
            shift = lax.rem(rank % 8 - me + 12, 8) - 4
            slot_d[slot] = jnp.where(used, rank // 8, 0)
            slot_r[slot] = jnp.where(used, anchor[2, ident] + PAD + 128 * shift, PAD)
            keep = reach < jnp.where(used, extent[ident], 0)
            lines = []
            for p in range(2):
                value = jnp.where(keep, p_ref[ident, pl.ds(8 * p, 8), :], 0.0)
                pm[slot, pl.ds(16 * p, 8), :] = value
                pm[slot, pl.ds(16 * p + 8, 8), :] = pltpu.roll(value, 64, 1)
                g0, g1 = coupling[2 * p, ident], coupling[2 * p + 1, ident]
                lines += [jnp.where(first_half, g0, g1), jnp.where(first_half, g1, g0)]
            four = jnp.where(low % 2 == 0, jnp.where(low < 2, lines[0], lines[2]), jnp.where(low < 2, lines[1], lines[3]))
            if q % 2 == 0:
                held = four
            else:
                gains[pl.ds(pl.multiple_of(32 * group, 32) + 4 * (q - 1), 8), :] = jnp.where(upper, held, four)
        return 0

    def unpack(d, _):
        for r in range(0, 96, 8):
            pair = vp_ref[d, pl.ds(r, 8), :]
            swapped = pltpu.roll(pair, 64, 1)
            v_ref[d, pl.ds(8 + 2 * r, 8, stride=2), :] = jnp.where(first_half, pair, swapped) + DIAG
            v_ref[d, pl.ds(9 + 2 * r, 8, stride=2), :] = jnp.where(first_half, swapped, pair) + DIAG
        return 0

    lax.fori_loop(0, G, unpack, 0)

    def apply(now, old, new, offset, base, rows, alpha, beta, count):
        def split(d, _):
            for r in range(0, rows, 16):
                v = now[d, pl.ds(base + r, 16), :]
                top = v.astype(BF16)
                hi[d, pl.ds(r, 16), :] = top
                lo[d, pl.ds(r, 16), :] = (v - top.astype(F32)).astype(BF16)
            return 0

        lax.fori_loop(0, G, split, 0)

        def stencil(it, _):
            px, py = it // 2, it % 2

            def dom(kx, ky):
                return 4 * lax.rem(px + kx, 4) + lax.rem(py + ky, 4)

            def pair(part, a, b):
                return jnp.concatenate([part[a, pl.ds(0, rows), :], part[b, pl.ds(0, rows), :]], axis=1)

            def stack(cases):
                return jnp.concatenate(
                    [jnp.concatenate([pair(part, *c) for part in (hi, lo) for c in case], axis=1) for case in cases],
                    axis=0,
                )

            lhs_x = stack([((dom(0, k), dom(2, k)), (dom(1, k), dom(3, k))) for k in (0, 2)])
            lhs_y = stack([((dom(k, 1), dom(k, 3)),) for k in (0, 2)])
            acc_x = jnp.dot(lhs_x, w_ref[pl.ds(0, 1024), :], preferred_element_type=F32)
            acc_y = jnp.dot(lhs_y, w_ref[pl.ds(1024, 512), :], preferred_element_type=F32)
            for kx in range(2):
                for ky in range(2):
                    d = dom(2 * kx, 2 * ky)
                    for r in range(0, rows, 8):
                        s = base + r
                        mid = now[d, pl.ds(s, 8), :]
                        val = acc_x[rows * ky + r : rows * ky + r + 8, 128 * kx : 128 * kx + 128]
                        val = val + acc_y[rows * kx + r : rows * kx + r + 8, 128 * ky : 128 * ky + 128]
                        val = val * (alpha * KIN / WSCALE)
                        val = val + (alpha * v_ref[d, pl.ds(s, 8), :]) * mid
                        for m in range(1, 7):
                            val = val + (alpha * KIN * STENCIL[m]) * (
                                now[d, pl.ds(s + m, 8), :] + now[d, pl.ds(s - m, 8), :]
                            )
                        if beta:
                            val = val - beta * old[d, pl.ds(s, 8), :]
                        new[d, pl.ds(s - offset, 8), :] = val
            return 0

        lax.fori_loop(0, 4, stencil, 0)

        if old is None:
            load.wait()
            lax.fori_loop(0, n_all // 8, prepare, 0)

        def project(group):
            for q in range(8):
                slot = 8 * group + q
                box = now[slot_d[slot], pl.ds(slot_r[slot], 8), :]
                for i in range(4):
                    prods[pl.ds(32 * q + 8 * i, 8), :] = pm[slot, pl.ds(8 * i, 8), :] * box
            out = []
            for t in range(4):
                v = prods[pl.ds(64 * t, 8, stride=8), :]
                for i in range(1, 8):
                    v = v + prods[pl.ds(64 * t + i, 8, stride=8), :]
                one = jnp.sum(jnp.where(first_half, v, 0.0), axis=1, keepdims=True)
                two = jnp.sum(jnp.where(first_half, 0.0, v), axis=1, keepdims=True)
                gain = gains[pl.ds(pl.multiple_of(32 * group, 32) + 8 * t, 8), :]
                out.append(alpha * gain * jnp.where(first_half, one, two))
            return tuple(out)

        def spread(group, coef):
            adds = []
            for q in range(8):
                slot = 8 * group + q
                w = None
                for i in range(4):
                    k = 4 * (q % 2) + i
                    piece = jnp.broadcast_to(coef[q // 2][k : k + 1, :], (8, 128))
                    term = pm[slot, pl.ds(8 * i, 8), :] * piece
                    w = term if w is None else w + term
                adds.append(w)
            for q in range(8):
                slot = 8 * group + q
                d, r = slot_d[slot], slot_r[slot] - offset
                new[d, pl.ds(r, 8), :] = new[d, pl.ds(r, 8), :] + adds[q]

        groups = count // 8

        def both_halves(group, coef):
            nxt = project(group)
            spread(group - 1, coef)
            return nxt

        @pl.when(groups > 0)
        def _():
            spread(groups - 1, lax.fori_loop(1, groups, both_halves, project(0)))

    plan = steps()
    chain = ((x_ref, None, bufb, 0, n_all), (bufb, x_ref, bufa, 0, n_all),
             (bufa, bufb, bufb, 0, n_all), (bufb, bufa, o_ref, PAD, n_own))
    for (now, old, new, offset, count), (base, rows), (alpha, beta) in zip(chain, RANGES, plan):
        apply(now, old, new, offset, base, rows, alpha, beta, count)


def run_filter(table, owner, anchor, extent, coupling, x, v, p, w):
    smem = pl.BlockSpec(memory_space=pltpu.SMEM)
    vmem = pl.BlockSpec(memory_space=pltpu.VMEM)
    return pl.pallas_call(
        filter_kernel,
        out_shape=jax.ShapeDtypeStruct((G, 128, 128), F32),
        in_specs=[smem] * 5 + [vmem] * 2 + [pl.BlockSpec(memory_space=pltpu.HBM), vmem],
        out_specs=vmem,
        scratch_shapes=[
            pltpu.VMEM((1024, 16, 128), F32),
            pltpu.VMEM((G, ROWS, 128), F32),
            pltpu.VMEM((G, ROWS, 128), F32),
            pltpu.VMEM((G, ROWS, 128), F32),
            pltpu.VMEM((G, RANGES[0][1], 128), BF16),
            pltpu.VMEM((G, RANGES[0][1], 128), BF16),
            pltpu.VMEM((SLOTS, 32, 128), F32),
            pltpu.VMEM((4 * SLOTS, 128), F32),
            pltpu.VMEM((256, 128), F32),
            pltpu.SMEM((SLOTS,), jnp.int32),
            pltpu.SMEM((SLOTS,), jnp.int32),
            pltpu.SemaphoreType.DMA,
        ],
        compiler_params=pltpu.CompilerParams(vmem_limit_bytes=56 * 2**20),
        name="chebyshev",
    )(table, owner, anchor, extent, coupling, x, v, p, w)


MESH = pl.DeviceIdType.MESH
PARTS = ((0, 48, 24, (0, 1, 2)), (48, 40, 24, (1, 2, 0)), (88, 40, 24, (2, 0, 1)))
V_PARTS = ((0, 32, 16, (0, 1)), (32, 32, 16, (1, 0)))


def position():
    return lax.axis_index("gx"), lax.axis_index("gy"), lax.axis_index("gz")


def plane_peer(offset):
    gx, gy, gz = position()
    return (lax.rem(gx + offset // 4, 4), lax.rem(gy + offset % 4, 4), gz)


def plane_source(offset):
    gx, gy, _ = position()
    return 4 * lax.rem(gx + 4 - offset // 4, 4) + lax.rem(gy + 4 - offset % 4, 4)


def line_peer(offset):
    gx, gy, gz = position()
    return (gx, gy, lax.rem(gz + offset, 8))


def greet():
    sem = pltpu.get_barrier_semaphore()

    def plane(o, _):
        pl.semaphore_signal(sem, inc=1, device_id=plane_peer(o), device_id_type=MESH)
        return 0

    def line(o, _):
        pl.semaphore_signal(sem, inc=1, device_id=line_peer(o), device_id_type=MESH)
        return 0

    lax.fori_loop(1, 16, plane, 0)
    lax.fori_loop(1, 8, line, 0)


def remote(src, dst, send, recv, target):
    return pltpu.make_async_remote_copy(
        src_ref=src, dst_ref=dst, send_sem=send, recv_sem=recv, device_id=target, device_id_type=MESH
    )


def pack(orb, pot, proj, perm, sent, vown, pown, cells, pair):
    first_half = lax.broadcasted_iota(jnp.int32, (16, 128), 1) < 64
    for q in range(G):
        sent[q] = orb[pl.ds(128 * q, 128), :].T
    pair[...] = pot[...].T
    vown[...] = jnp.concatenate([pair[pl.ds(0, 64, stride=2), :], pair[pl.ds(1, 64, stride=2), :]], axis=1)
    x = proj[...]
    top = x.astype(BF16)
    rest = x - top.astype(F32)
    mid = rest.astype(BF16)
    low = (rest - mid.astype(F32)).astype(BF16)
    parts = jnp.dot(jnp.concatenate([top, mid, low], axis=0), perm[...], preferred_element_type=F32)
    moved = (parts[:32] + parts[32:64]) + parts[64:]
    for t in range(4):
        cells[t] = moved[:, 128 * t : 128 * t + 128]
    for t in range(4):
        even, odd = cells[t, pl.ds(0, 16, stride=2), :], cells[t, pl.ds(1, 16, stride=2), :]
        pown[pl.ds(2 * t, 16, stride=8), :] = jnp.where(first_half, even, pltpu.roll(odd, 64, 1))
        pown[pl.ds(2 * t + 1, 16, stride=8), :] = jnp.where(first_half, pltpu.roll(even, 64, 1), odd)


def list_atoms(owner, anchor, gz):
    rank = owner[...]
    z = jnp.concatenate([anchor[2:3, 128 * r : 128 * r + 128] for r in range(8)], axis=0)
    slab = rank % 8
    own = slab == gz
    near = ((slab == (gz + 7) % 8) & (z + MARGIN >= 128)) | ((slab == (gz + 1) % 8) & (z + B <= MARGIN))
    row = lax.broadcasted_iota(jnp.int32, (128, 128), 0)
    col = lax.broadcasted_iota(jnp.int32, (128, 128), 1)
    sub = lax.broadcasted_iota(jnp.int32, (8, 128), 0)
    before = (row < col).astype(F32)

    def ranks(mask):
        m = mask.astype(F32)
        inside = jnp.dot(m.astype(BF16), before.astype(BF16), preferred_element_type=F32)
        counts = jnp.sum(m, axis=1, keepdims=True)
        base = jnp.zeros((1, 1), F32)
        bases = []
        for r in range(8):
            bases.append(base)
            base = base + counts[r : r + 1]
        return inside + jnp.concatenate(bases, axis=0), base

    at_own, n_own = ranks(own)
    at_near, n_near = ranks(near)
    first = jnp.floor((n_own + 7.0) * 0.125) * 8.0
    last = first + jnp.floor((n_near + 7.0) * 0.125) * 8.0
    at = jnp.where(own, at_own, jnp.where(near, at_near + first, -1.0)).astype(jnp.int32)
    high = jnp.where(at >= 0, at // 128, -1)
    low = (at % 128).astype(F32).T
    ident = 128 * sub + lax.broadcasted_iota(jnp.int32, (8, 128), 1) + 1
    slot_row = lax.broadcasted_iota(jnp.int32, (16, 128), 0)
    big = jnp.zeros((16, 128), F32)
    small = jnp.zeros((16, 128), F32)
    for r in range(8):
        hit = slot_row == high[r : r + 1]
        right = (low[:, r : r + 1] == col.astype(F32)).astype(BF16)
        one = ident[r : r + 1]
        big = big + jnp.dot(jnp.where(hit, (one // 32).astype(F32), 0.0).astype(BF16), right, preferred_element_type=F32)
        small = small + jnp.dot(jnp.where(hit, (one % 32).astype(F32), 0.0).astype(BF16), right, preferred_element_type=F32)
    table = big * 32.0 + small
    lane = lax.broadcasted_iota(jnp.int32, (16, 128), 1)
    table = jnp.where(slot_row == 15, jnp.where(lane == 0, first, jnp.where(lane == 1, last, 0.0)), table)
    return table.astype(jnp.int32)


def gather_kernel(
    orb, pot, proj, perm, owner, anchor, x_out, v_out, p_out, table,
    sent, vown, pown, cells, pair,
    a2a_send, a2a_recv, p_send, p_recv, v_send, v_recv, twin_send, twin_recv, halo_send, halo_recv, here,
):
    gx, gy, gz = position()
    y, core = gz // 2, gz % 2
    mine = 4 * gx + gy
    greet()
    pack(orb, pot, proj, perm, sent, vown, pown, cells, pair)
    pl.semaphore_wait(pltpu.get_barrier_semaphore(), 22)
    local = [
        pltpu.make_async_copy(pown, p_out.at[gx, gy, y, core], here.at[0]),
        pltpu.make_async_copy(vown, v_out.at[gx, gy, pl.ds(16, 64)], here.at[1]),
        pltpu.make_async_copy(sent.at[mine], x_out.at[mine, pl.ds(PAD, 128)], here.at[2]),
    ]
    for copy in local:
        copy.start()
    where = (gx, gy, y)

    def near(dim, step):
        return lax.rem(where[dim] + step + 4, 4)

    def neighbour(dim, step):
        at = list(where)
        at[dim] = near(dim, step)
        return (at[0], at[1], 2 * at[2] + core)

    def p_view(part, at2, at3, rows, at1=None):
        start, _, _, (d1, d2, d3) = PARTS[part]
        idx = [None, None, None]
        idx[d1] = pl.ds(0, 4) if at1 is None else at1
        idx[d2] = at2
        idx[d3] = at3
        return p_out.at[idx[0], idx[1], idx[2], core, pl.ds(start + rows[0], rows[1])]

    def v_view(held, dim, at, start, rows):
        idx = [pl.ds(0, 4) if k in held else where[k] for k in range(2)]
        idx[dim] = at
        return v_out.at[idx[0], idx[1], pl.ds(16 + start, rows)]

    used = [0, 0, 0]

    def p_copy(part, src, dim, step):
        k = used[part]
        used[part] += 1
        return remote(src, src, p_send.at[part, k], p_recv.at[part, k], neighbour(dim, step))

    partner = (gx, gy, gz + 1 - 2 * core)
    twins = []

    def twin(part, at2, at3):
        k = sum(1 for t in twins if t[0] == part)
        src = p_view(part, at2, at3, (0, PARTS[part][1]))
        copy = remote(src, src, twin_send.at[part, k], twin_recv.at[part, k], partner)
        copy.start()
        twins.append((part, copy))

    def start(copies):
        for copy in copies:
            copy.start()
        return copies

    def wait(copies):
        for copy in copies:
            copy.wait()

    def a2a(o):
        peer = plane_peer(o)
        return remote(
            sent.at[4 * peer[0] + peer[1]], x_out.at[mine, pl.ds(PAD, 128)], a2a_send.at[o], a2a_recv.at[o], peer
        )

    def send_a2a(lo_o, hi_o):
        def step(o, _):
            a2a(o).start()
            return 0

        lax.fori_loop(lo_o, hi_o, step, 0)

    def v_copies(phase, second):
        out = []
        for i, (at, rows, half, order) in enumerate(V_PARTS):
            dim, held = order[phase], order[:phase]
            base = 4 * phase
            if not second:
                own = v_view(held, dim, where[dim], at, rows)
                for k, step in ((0, 1), (1, -1)):
                    out.append(remote(own, own, v_send.at[i, base + k], v_recv.at[i, base + k], neighbour(dim, step)))
            else:
                for k, step, lo_r, n_r in ((2, 1, 0, half), (3, -1, half, rows - half)):
                    src = v_view(held, dim, near(dim, -step), at + lo_r, n_r)
                    out.append(remote(src, src, v_send.at[i, base + k], v_recv.at[i, base + k], neighbour(dim, step)))
        return out

    def along3(part, at2):
        d3 = PARTS[part][3][2]
        src = p_view(part, at2, where[d3], (0, PARTS[part][1]))
        return [p_copy(part, src, d3, 1), p_copy(part, src, d3, -1)]

    def forward3(part, at2):
        rows, half, d3 = PARTS[part][1], PARTS[part][2], PARTS[part][3][2]
        return [
            p_copy(part, p_view(part, at2, near(d3, -1), (0, half)), d3, 1),
            p_copy(part, p_view(part, at2, near(d3, 1), (half, rows - half)), d3, -1),
        ]

    three = range(3)
    dims = [part[3] for part in PARTS]
    wait(local)

    m1 = []
    for i in three:
        d1, d2, d3 = dims[i]
        own = p_view(i, where[d2], where[d3], (0, PARTS[i][1]), where[d1])
        m1 += [p_copy(i, own, d1, 1), p_copy(i, own, d1, -1)]
    start(m1)
    v = start(v_copies(0, False))
    send_a2a(1, 4)
    wait(m1)
    m2 = []
    for i in three:
        d1, d2, d3 = dims[i]
        rows, half = PARTS[i][1], PARTS[i][2]
        m2 += [
            p_copy(i, p_view(i, where[d2], where[d3], (0, half), near(d1, -1)), d1, 1),
            p_copy(i, p_view(i, where[d2], where[d3], (half, rows - half), near(d1, 1)), d1, -1),
        ]
    start(m2)
    wait(v)
    v = start(v_copies(0, True))
    send_a2a(4, 7)
    wait(m2)
    s3 = []
    for i in three:
        d1, d2, d3 = dims[i]
        row = p_view(i, where[d2], where[d3], (0, PARTS[i][1]))
        s3 += [p_copy(i, row, d2, 1), p_copy(i, row, d2, -1)]
    start(s3)
    a5 = start([c for i in three for c in along3(i, where[dims[i][1]])])
    for i in three:
        twin(i, where[dims[i][1]], where[dims[i][2]])
    wait(v)
    v = start(v_copies(1, False))
    send_a2a(7, 10)
    wait(s3)
    s4 = []
    for i in three:
        d1, d2, d3 = dims[i]
        rows, half = PARTS[i][1], PARTS[i][2]
        s4 += [
            p_copy(i, p_view(i, near(d2, -1), where[d3], (0, half)), d2, 1),
            p_copy(i, p_view(i, near(d2, 1), where[d3], (half, rows - half)), d2, -1),
        ]
    start(s4)
    b5 = start([c for i in three for k in (1, -1) for c in along3(i, near(dims[i][1], k))])
    for i in three:
        for k in (1, -1):
            twin(i, near(dims[i][1], k), where[dims[i][2]])
    wait(v)
    v = start(v_copies(1, True))
    wait(a5)
    a6 = start([c for i in three for c in forward3(i, where[dims[i][1]])])
    for i in three:
        for k in (1, -1):
            twin(i, where[dims[i][1]], near(dims[i][2], k))
    send_a2a(10, 13)
    wait(s4)
    c5 = start([c for i in three for c in along3(i, near(dims[i][1], 2))])
    for i in three:
        twin(i, near(dims[i][1], 2), where[dims[i][2]])
    send_a2a(13, 16)
    wait(v)
    right, left = line_peer(1), line_peer(7)
    whole = pl.ds(0, 4)
    halos = start([
        remote(v_out.at[whole, whole, pl.ds(64, 16)], v_out.at[whole, whole, pl.ds(0, 16)],
               halo_send.at[2], halo_recv.at[2], right),
        remote(v_out.at[whole, whole, pl.ds(16, 16)], v_out.at[whole, whole, pl.ds(80, 16)],
               halo_send.at[3], halo_recv.at[3], left),
    ])
    wait(b5)
    b6 = start([c for i in three for k in (1, -1) for c in forward3(i, near(dims[i][1], k))])
    for i in three:
        for m in (1, -1):
            for k in (1, -1):
                twin(i, near(dims[i][1], m), near(dims[i][2], k))
    table[...] = list_atoms(owner, anchor, gz)
    wait(a6)
    for i in three:
        twin(i, where[dims[i][1]], near(dims[i][2], 2))
    wait(c5)
    c6 = start([c for i in three for c in forward3(i, near(dims[i][1], 2))])
    for i in three:
        for k in (1, -1):
            twin(i, near(dims[i][1], 2), near(dims[i][2], k))

    def finish_a2a(o, _):
        a2a(o).wait()
        return 0

    lax.fori_loop(1, 16, finish_a2a, 0)
    halos += start([
        remote(x_out.at[pl.ds(0, G), pl.ds(PAD + 128 - HALO, HALO)], x_out.at[pl.ds(0, G), pl.ds(PAD - HALO, HALO)],
               halo_send.at[0], halo_recv.at[0], right),
        remote(x_out.at[pl.ds(0, G), pl.ds(PAD, HALO)], x_out.at[pl.ds(0, G), pl.ds(PAD + 128, HALO)],
               halo_send.at[1], halo_recv.at[1], left),
    ])
    wait(b6)
    for i in three:
        for k in (1, -1):
            twin(i, near(dims[i][1], k), near(dims[i][2], 2))
    wait(c6)
    for i in three:
        twin(i, near(dims[i][1], 2), near(dims[i][2], 2))
    wait(halos)
    wait([copy for _, copy in twins])


def permutation():
    at = np.arange(512)
    perm = np.zeros((512, 512), np.float32)
    perm[at, (at % 8) * 64 + at // 8] = 1.0
    return perm


def run_gather(orb, pot, proj, perm, owner, anchor):
    vmem = pl.BlockSpec(memory_space=pltpu.VMEM)
    hbm = pl.BlockSpec(memory_space=pltpu.HBM)
    dma = pltpu.SemaphoreType.DMA
    return pl.pallas_call(
        gather_kernel,
        out_shape=(
            jax.ShapeDtypeStruct((G, ROWS, 128), F32),
            jax.ShapeDtypeStruct((4, 4, 96, 128), F32),
            jax.ShapeDtypeStruct((4, 4, 4, 2, 128, 128), F32),
            jax.ShapeDtypeStruct((16, 128), jnp.int32),
        ),
        in_specs=[vmem] * 6,
        out_specs=(hbm, hbm, hbm, vmem),
        scratch_shapes=[
            pltpu.VMEM((G, 128, 128), F32),
            pltpu.VMEM((64, 128), F32),
            pltpu.VMEM((128, 128), F32),
            pltpu.VMEM((4, 32, 128), F32),
            pltpu.VMEM((128, 64), F32),
            dma((16,)), dma((16,)), dma((3, 24)), dma((3, 24)), dma((2, 8)), dma((2, 8)),
            dma((3, 16)), dma((3, 16)), dma((4,)), dma((4,)), dma((3,)),
        ],
        compiler_params=pltpu.CompilerParams(collective_id=1, has_side_effects=True),
        name="gather",
    )(orb, pot, proj, perm, owner, anchor)


def return_kernel(
    y, out, total, recv, gram_a, gram_b, a2a_send, a2a_recv, a_send, a_recv, b_send, b_recv, here,
):
    gx, gy, gz = position()
    mine = 4 * gx + gy
    own = pltpu.make_async_copy(y.at[mine], recv.at[mine], here.at[0])
    own.start()
    greet()
    pl.semaphore_wait(pltpu.get_barrier_semaphore(), 22)

    def a2a(o):
        peer = plane_peer(o)
        return remote(
            y.at[4 * peer[0] + peer[1]], recv.at[mine], a2a_send.at[o], a2a_recv.at[o], peer
        )

    def send(o, _):
        a2a(o).start()
        return 0

    lax.fori_loop(1, 16, send, 0)

    def place(source):
        out[pl.ds(pl.multiple_of(128 * source, 128), 128), :] = recv[source].T

    own.wait()
    place(mine)

    def receive(o, _):
        a2a(o).wait()
        place(plane_source(o))
        return 0

    lax.fori_loop(1, 16, receive, 0)

    def gram(c, acc):
        cells = jnp.concatenate([out[pl.ds(8 * c + i, 32, stride=64), :] for i in range(8)], axis=1)
        top = cells.astype(BF16)
        rest = (cells - top.astype(F32)).astype(BF16)
        both = jnp.concatenate([top, rest], axis=0)
        return acc + lax.dot_general(both, both, (((1,), (1,)), ((), ())), preferred_element_type=F32)

    acc = lax.fori_loop(0, 8, gram, jnp.zeros((64, 64), F32))
    g = acc[:32, :32] + (acc[:32, 32:] + acc[32:, :32])
    gram_a[mine] = jnp.concatenate([g[8 * b : 8 * b + 8] for b in range(4)], axis=1)

    def plane(o):
        return remote(gram_a.at[mine], gram_a.at[mine], a_send.at[o], a_recv.at[o], plane_peer(o))

    def line(o):
        return remote(gram_b.at[gz], gram_b.at[gz], b_send.at[o], b_recv.at[o], line_peer(o))

    def start_plane(o, _):
        plane(o).start()
        return 0

    def wait_plane(o, _):
        plane(o).wait()
        return 0

    def start_line(o, _):
        line(o).start()
        return 0

    def wait_line(o, _):
        line(o).wait()
        return 0

    lax.fori_loop(1, 16, start_plane, 0)
    lax.fori_loop(1, 16, wait_plane, 0)
    acc = gram_a[0]
    for i in range(1, 16):
        acc = acc + gram_a[i]
    gram_b[gz] = acc
    lax.fori_loop(1, 8, start_line, 0)
    lax.fori_loop(1, 8, wait_line, 0)
    acc = gram_b[0]
    for i in range(1, 8):
        acc = acc + gram_b[i]
    acc = acc * (1.0 / (32 * 32 * 1024))
    for b in range(4):
        total[pl.ds(8 * b, 8), :] = acc[:, 32 * b : 32 * b + 32]


def run_return(y):
    vmem = pl.BlockSpec(memory_space=pltpu.VMEM)
    dma = pltpu.SemaphoreType.DMA
    return pl.pallas_call(
        return_kernel,
        out_shape=(jax.ShapeDtypeStruct((2048, 128), F32), jax.ShapeDtypeStruct((32, 32), F32)),
        in_specs=[vmem],
        out_specs=(vmem, vmem),
        scratch_shapes=[
            pltpu.VMEM((G, 128, 128), F32),
            pltpu.VMEM((G, 8, 128), F32),
            pltpu.VMEM((8, 8, 128), F32),
            dma((16,)), dma((16,)), dma((16,)), dma((16,)), dma((8,)), dma((8,)), dma((1,)),
        ],
        compiler_params=pltpu.CompilerParams(collective_id=2, has_side_effects=True),
        name="giveback",
    )(y)


def body(orbitals, potential, projectors, owner_rank, box_anchor, box_extent, coupling):
    perm = jnp.asarray(permutation()).astype(BF16)
    x, v, p, table = run_gather(
        orbitals.reshape(2048, 128), potential.reshape(64, 128), projectors.reshape(32, 512), perm,
        owner_rank.reshape(8, 128), box_anchor,
    )
    w = jnp.asarray(weights()).astype(BF16)
    y = run_filter(
        table, owner_rank, box_anchor, box_extent, coupling.T,
        x, v.reshape(G, 96, 128), p.reshape(1024, 16, 128), w,
    )
    filtered, total = run_return(y)
    return filtered.reshape(orbitals.shape), total


def solution(mesh):
    return jax.shard_map(
        body,
        mesh=mesh,
        in_specs=(
            P(None, "gx", "gy", "gz"),
            P("gx", "gy", "gz"),
            P(("gx", "gy", "gz"), None, None),
            P(),
            P(),
            P(),
            P(),
        ),
        out_specs=(P(None, "gx", "gy", "gz"), P()),
        check_vma=False,
    )
```

time: 159 us -> 129 us (0.81); the launches traced: 161 us -> 128 us
  Pallas kernels: 144 us -> 122 us
  local copies, waits for them, and re-layouts: 11.3 us -> 5.12 us
  other arithmetic: 3.49 us -> 0 us
    pallas_call x1, Pallas kernels: 51.6 us -> 31.7 us  [run_filter(): pl.pallas_call(filter_kernel, out_shape=jax.ShapeDtypeStruct((G, 128, 128...]
    pallas_call x1, Pallas kernels: 60.9 us -> 52.8 us  [run_gather(): pl.pallas_call(gather_kernel, out_shape=(jax.ShapeDtypeStruct((G, ROWS, 1...]
    pallas_call x1, Pallas kernels: 31.8 us -> 37.6 us  [run_return(): pl.pallas_call(return_kernel, out_shape=(jax.ShapeDtypeStruct((2048, 128)...]
    reshape x6 -> x1, local copies, waits for them, and re-layouts: 5.52 us -> 1.49 us  [body(): projectors.reshape(32, 512)]
    reduce_sum x3 -> x0, other arithmetic: 2.92 us -> none  [the longest x1 1.42 us: slots(): n_all = first + (jnp.sum(near.astype(jnp.int32)) + 7) // 8 * 8]
    unnamed x10 -> x2, local copies, waits for them, and re-layouts: 4.72 us -> 3.63 us
where the time goes in v3:
time: 129 us; the launch traced here: 128 us
  Pallas kernels  122 us (95%)
  local copies, waits for them, and re-layouts  5.12 us (4%)
    pallas_call x1, Pallas kernels, run_gather(): pl.pallas_call(gather_kernel, out_shape=(jax.ShapeDtypeStruct((G, ROWS, 1...  52.8 us
    pallas_call x1, Pallas kernels, run_return(): pl.pallas_call(return_kernel, out_shape=(jax.ShapeDtypeStruct((2048, 128)...  37.6 us
    pallas_call x1, Pallas kernels, run_filter(): pl.pallas_call(filter_kernel, out_shape=jax.ShapeDtypeStruct((G, 128, 128...  31.7 us
    unnamed x2, local copies, waits for them, and re-layouts  3.63 us

profile of v3, /device:TPU:1, one launch (start us, length us, event | category | flops | bytes accessed | tf_op | source)
XLA Modules:
  0.0 127.9 jit_solution(4211748543862866781)
XLA Ops:
  0.6 1.5 %reshape.27.proj = f32[32,512]{1,0:T(8,128)} reshape(f32[8,4,512]{2,1,0:T(4,128)} %param.11) | data formatting | bytes 131072 | tf_op jit(solution)/shard_map/reshape | solution.py:731
  2.1 52.8 %gather.1 = (f32[16,208,128]{2,1,0:T(8,128)}, f32[4,4,96,128]{3,2,1,0:T(8,128)}, f32[4,4,4,2,128,128]{5,4,3,2,1,0:T(8,128)}, s32[16,128]{1,0:T(8,128)}) custom-call(f32[2048,128]{1,0:T(8,128)} %bitcast.8, f32[64,128]{1,0:T(8,128)} %bitcast.11, f32[32,512]{1,0:T(8,128)} %reshape.27.proj, bf16[512,512]{1,0:T(8,128)(2,1)} %constant.7.perm, s32[8,128]{1,0:T(8,128)} %bitcast.13, ...), custom_call_target="tpu_custom_call" | custom-call | tf_op jit(solution)/shard_map/gather/pallas_call | solution.py:601
  54.9 31.7 %chebyshev.1.y = f32[16,128,128]{2,1,0:T(8,128)} custom-call(s32[16,128]{1,0:T(8,128)} %get-tuple-element.8.table, s32[1024]{0:T(1024)} %owner.1, s32[3,1024]{1,0:T(4,128)} %anchor.3, s32[1024]{0:T(1024)} %extent.1, f32[4,1024]{1,0:T(4,128)} %bitcast.12, f32[16,208,128]{2,1,0:T(8,128)} %get-tuple-element.9.x_ref, f32[16,96,128]{2,1,0:T(8,128)} %bitcast.10, ...), custom_call_target="tpu_custom_call" | custom-call | tf_op jit(solution)/shard_map/chebyshev/pallas_call | solution.py:236
  86.7 37.6 %giveback.1 = (f32[2048,128]{1,0:T(8,128)}, f32[32,32]{1,0:T(8,128)}) custom-call(f32[16,128,128]{2,1,0:T(8,128)} %chebyshev.1.y), custom_call_target="tpu_custom_call" | custom-call | tf_op jit(solution)/shard_map/giveback/pallas_call | solution.py:712
  124.2 2.3 %copy.13 = f32[32,8,8,128]{3,2,1,0:T(8,128)} copy(f32[32,8,8,128]{3,2,1,0:T(8,128)} %bitcast.9) | data formatting | bytes 2097152
  126.6 1.3 %copy.14 = f32[32,32]{1,0:T(8,128)} copy(f32[32,32]{1,0:T(8,128)} %get-tuple-element.17) | data formatting | bytes 8192

commit v4 on v3

--- a/solution.py
+++ b/solution.py
@@ -35,7 +35,8 @@
 WSCALE = 35.0 / 32.0
 KIN = -0.5 / (SPACING * SPACING)
 DIAG = KIN * 3.0 * STENCIL[0] - MIDDLE
-SLOTS = 1040
+GROUP = 16
+SLOTS = 1024 + 2 * GROUP
 F32 = jnp.float32
 BF16 = jnp.bfloat16
 
@@ -73,9 +74,9 @@
 
 
 def filter_kernel(
-    table, owner, anchor, extent, coupling,
+    table, coupling,
     x_ref, vp_ref, p_hbm, w_ref, o_ref,
-    p_ref, v_ref, bufa, bufb, hi, lo, pm, gains, prods, slot_d, slot_r, load_sem,
+    p_ref, v_ref, bufa, bufb, hi, lo, acc_x, acc_y, pm, gains, prods, load_sem,
 ):
     lane = lax.broadcasted_iota(jnp.int32, (8, 128), 1)
     sub = lax.broadcasted_iota(jnp.int32, (8, 128), 0)
@@ -83,35 +84,35 @@
     upper = sub < 4
     low = sub % 4
     reach = jnp.maximum(jnp.maximum((lane % 64) // 8, lane % 8), sub)
-    me = lax.axis_index("gz")
     n_own, n_all = table[15, 0], table[15, 1]
 
     load = pltpu.make_async_copy(p_hbm, p_ref, load_sem)
     load.start()
 
+    def place(group):
+        per_row = 128 // GROUP
+        return group // per_row, GROUP * lax.rem(group, per_row)
+
     def prepare(group, _):
-        for q in range(8):
-            slot = 8 * group + q
-            ident = table[slot // 128, slot % 128] - 1
-            used = ident >= 0
-            ident = jnp.maximum(ident, 0)
-            rank = owner[ident]
-            shift = lax.rem(rank % 8 - me + 12, 8) - 4
-            slot_d[slot] = jnp.where(used, rank // 8, 0)
-            slot_r[slot] = jnp.where(used, anchor[2, ident] + PAD + 128 * shift, PAD)
-            keep = reach < jnp.where(used, extent[ident], 0)
+        row, at = place(group)
+        fours = []
+        for q in range(GROUP):
+            slot = GROUP * group + q
+            ident = jnp.maximum(table[row, at + q] - 1, 0)
+            keep = reach < table[48 + row, at + q]
+            g = [coupling[k, ident] for k in range(4)]
             lines = []
             for p in range(2):
                 value = jnp.where(keep, p_ref[ident, pl.ds(8 * p, 8), :], 0.0)
                 pm[slot, pl.ds(16 * p, 8), :] = value
                 pm[slot, pl.ds(16 * p + 8, 8), :] = pltpu.roll(value, 64, 1)
-                g0, g1 = coupling[2 * p, ident], coupling[2 * p + 1, ident]
-                lines += [jnp.where(first_half, g0, g1), jnp.where(first_half, g1, g0)]
-            four = jnp.where(low % 2 == 0, jnp.where(low < 2, lines[0], lines[2]), jnp.where(low < 2, lines[1], lines[3]))
-            if q % 2 == 0:
-                held = four
-            else:
-                gains[pl.ds(pl.multiple_of(32 * group, 32) + 4 * (q - 1), 8), :] = jnp.where(upper, held, four)
+                lines += [jnp.where(first_half, g[2 * p], g[2 * p + 1]), jnp.where(first_half, g[2 * p + 1], g[2 * p])]
+            even, odd = jnp.where(low < 2, lines[0], lines[2]), jnp.where(low < 2, lines[1], lines[3])
+            fours.append(jnp.where(low % 2 == 0, even, odd))
+        for t in range(GROUP // 2):
+            gains[pl.ds(pl.multiple_of(4 * GROUP * group, 64) + 8 * t, 8), :] = jnp.where(
+                upper, fours[2 * t], fours[2 * t + 1]
+            )
         return 0
 
     def unpack(d, _):
@@ -135,7 +136,7 @@
 
         lax.fori_loop(0, G, split, 0)
 
-        def stencil(it, _):
+        def multiply(it):
             px, py = it // 2, it % 2
 
             def dom(kx, ky):
@@ -152,16 +153,19 @@
 
             lhs_x = stack([((dom(0, k), dom(2, k)), (dom(1, k), dom(3, k))) for k in (0, 2)])
             lhs_y = stack([((dom(k, 1), dom(k, 3)),) for k in (0, 2)])
-            acc_x = jnp.dot(lhs_x, w_ref[pl.ds(0, 1024), :], preferred_element_type=F32)
-            acc_y = jnp.dot(lhs_y, w_ref[pl.ds(1024, 512), :], preferred_element_type=F32)
+            acc_x[pl.ds(0, 2 * rows), :] = jnp.dot(lhs_x, w_ref[pl.ds(0, 1024), :], preferred_element_type=F32)
+            acc_y[pl.ds(0, 2 * rows), :] = jnp.dot(lhs_y, w_ref[pl.ds(1024, 512), :], preferred_element_type=F32)
+
+        def finish(it):
+            px, py = it // 2, it % 2
             for kx in range(2):
                 for ky in range(2):
-                    d = dom(2 * kx, 2 * ky)
+                    d = 4 * (px + 2 * kx) + py + 2 * ky
                     for r in range(0, rows, 8):
                         s = base + r
                         mid = now[d, pl.ds(s, 8), :]
-                        val = acc_x[rows * ky + r : rows * ky + r + 8, 128 * kx : 128 * kx + 128]
-                        val = val + acc_y[rows * kx + r : rows * kx + r + 8, 128 * ky : 128 * ky + 128]
+                        val = acc_x[pl.ds(rows * ky + r, 8), pl.ds(128 * kx, 128)]
+                        val = val + acc_y[pl.ds(rows * kx + r, 8), pl.ds(128 * ky, 128)]
                         val = val * (alpha * KIN / WSCALE)
                         val = val + (alpha * v_ref[d, pl.ds(s, 8), :]) * mid
                         for m in range(1, 7):
@@ -171,57 +175,72 @@
                         if beta:
                             val = val - beta * old[d, pl.ds(s, 8), :]
                         new[d, pl.ds(s - offset, 8), :] = val
+
+        def both_parts(it, _):
+            finish(it)
+            multiply(it + 1)
             return 0
 
-        lax.fori_loop(0, 4, stencil, 0)
+        multiply(0)
+        lax.fori_loop(0, 3, both_parts, 0)
+        finish(3)
 
         if old is None:
             load.wait()
-            lax.fori_loop(0, n_all // 8, prepare, 0)
+            lax.fori_loop(0, n_all // GROUP, prepare, 0)
 
         def project(group):
-            for q in range(8):
-                slot = 8 * group + q
-                box = now[slot_d[slot], pl.ds(slot_r[slot], 8), :]
+            row, at = place(group)
+            for q in range(GROUP):
+                box = now[table[16 + row, at + q], pl.ds(table[32 + row, at + q], 8), :]
                 for i in range(4):
-                    prods[pl.ds(32 * q + 8 * i, 8), :] = pm[slot, pl.ds(8 * i, 8), :] * box
+                    prods[pl.ds(32 * q + 8 * i, 8), :] = pm[GROUP * group + q, pl.ds(8 * i, 8), :] * box
             out = []
-            for t in range(4):
-                v = prods[pl.ds(64 * t, 8, stride=8), :]
-                for i in range(1, 8):
-                    v = v + prods[pl.ds(64 * t + i, 8, stride=8), :]
+            for t in range(GROUP // 2):
+                v = [prods[pl.ds(64 * t + i, 8, stride=8), :] for i in range(8)]
+                while len(v) > 1:
+                    v = [v[i] + v[i + 1] for i in range(0, len(v), 2)]
+                out.append(v[0])
+            return tuple(out)
+
+        def weigh(group, sums):
+            out = []
+            for t in range(GROUP // 2):
+                v = sums[t]
                 one = jnp.sum(jnp.where(first_half, v, 0.0), axis=1, keepdims=True)
                 two = jnp.sum(jnp.where(first_half, 0.0, v), axis=1, keepdims=True)
-                gain = gains[pl.ds(pl.multiple_of(32 * group, 32) + 8 * t, 8), :]
+                gain = gains[pl.ds(pl.multiple_of(4 * GROUP * group, 64) + 8 * t, 8), :]
                 out.append(alpha * gain * jnp.where(first_half, one, two))
             return tuple(out)
 
         def spread(group, coef):
+            row, at = place(group)
             adds = []
-            for q in range(8):
-                slot = 8 * group + q
-                w = None
+            for q in range(GROUP):
+                terms = []
                 for i in range(4):
                     k = 4 * (q % 2) + i
                     piece = jnp.broadcast_to(coef[q // 2][k : k + 1, :], (8, 128))
-                    term = pm[slot, pl.ds(8 * i, 8), :] * piece
-                    w = term if w is None else w + term
-                adds.append(w)
-            for q in range(8):
-                slot = 8 * group + q
-                d, r = slot_d[slot], slot_r[slot] - offset
+                    terms.append(pm[GROUP * group + q, pl.ds(8 * i, 8), :] * piece)
+                adds.append((terms[0] + terms[1]) + (terms[2] + terms[3]))
+            for q in range(GROUP):
+                d, r = table[16 + row, at + q], table[32 + row, at + q] - offset
                 new[d, pl.ds(r, 8), :] = new[d, pl.ds(r, 8), :] + adds[q]
 
-        groups = count // 8
-
-        def both_halves(group, coef):
+        groups = count // GROUP
+
+        def stages(group, carry):
+            sums, coef = carry
             nxt = project(group)
-            spread(group - 1, coef)
-            return nxt
+            spread(jnp.maximum(group - 2, 0), coef)
+            return nxt, weigh(group - 1, sums)
 
         @pl.when(groups > 0)
         def _():
-            spread(groups - 1, lax.fori_loop(1, groups, both_halves, project(0)))
+            none = tuple(jnp.zeros((8, 128), F32) for _ in range(GROUP // 2))
+            sums, coef = lax.fori_loop(1, groups, stages, (project(0), none))
+            spread(jnp.maximum(groups - 2, 0), coef)
+            spread(groups - 1, weigh(groups - 1, sums))
 
     plan = steps()
     chain = ((x_ref, None, bufb, 0, n_all), (bufb, x_ref, bufa, 0, n_all),
@@ -230,13 +249,13 @@
         apply(now, old, new, offset, base, rows, alpha, beta, count)
 
 
-def run_filter(table, owner, anchor, extent, coupling, x, v, p, w):
+def run_filter(table, coupling, x, v, p, w):
     smem = pl.BlockSpec(memory_space=pltpu.SMEM)
     vmem = pl.BlockSpec(memory_space=pltpu.VMEM)
     return pl.pallas_call(
         filter_kernel,
         out_shape=jax.ShapeDtypeStruct((G, 128, 128), F32),
-        in_specs=[smem] * 5 + [vmem] * 2 + [pl.BlockSpec(memory_space=pltpu.HBM), vmem],
+        in_specs=[smem] * 2 + [vmem] * 2 + [pl.BlockSpec(memory_space=pltpu.HBM), vmem],
         out_specs=vmem,
         scratch_shapes=[
             pltpu.VMEM((1024, 16, 128), F32),
@@ -245,20 +264,21 @@
             pltpu.VMEM((G, ROWS, 128), F32),
             pltpu.VMEM((G, RANGES[0][1], 128), BF16),
             pltpu.VMEM((G, RANGES[0][1], 128), BF16),
+            pltpu.VMEM((2 * RANGES[0][1], 256), F32),
+            pltpu.VMEM((2 * RANGES[0][1], 256), F32),
             pltpu.VMEM((SLOTS, 32, 128), F32),
             pltpu.VMEM((4 * SLOTS, 128), F32),
-            pltpu.VMEM((256, 128), F32),
-            pltpu.SMEM((SLOTS,), jnp.int32),
-            pltpu.SMEM((SLOTS,), jnp.int32),
+            pltpu.VMEM((32 * GROUP, 128), F32),
             pltpu.SemaphoreType.DMA,
         ],
         compiler_params=pltpu.CompilerParams(vmem_limit_bytes=56 * 2**20),
         name="chebyshev",
-    )(table, owner, anchor, extent, coupling, x, v, p, w)
+    )(table, coupling, x, v, p, w)
 
 
 MESH = pl.DeviceIdType.MESH
-PARTS = ((0, 48, 24, (0, 1, 2)), (48, 40, 24, (1, 2, 0)), (88, 40, 24, (2, 0, 1)))
+PARTS = ((0, 24, 16, (0, 1, 2)), (24, 24, 16, (1, 0, 2)), (48, 40, 24, (1, 2, 0)), (88, 40, 24, (0, 2, 1)))
+A2A_CUTS = (9, 16)
 V_PARTS = ((0, 32, 16, (0, 1)), (32, 32, 16, (1, 0)))
 
 
@@ -308,7 +328,7 @@
         sent[q] = orb[pl.ds(128 * q, 128), :].T
     pair[...] = pot[...].T
     vown[...] = jnp.concatenate([pair[pl.ds(0, 64, stride=2), :], pair[pl.ds(1, 64, stride=2), :]], axis=1)
-    x = proj[...]
+    x = jnp.concatenate([proj[a] for a in range(8)], axis=0)
     top = x.astype(BF16)
     rest = x - top.astype(F32)
     mid = rest.astype(BF16)
@@ -323,7 +343,7 @@
         pown[pl.ds(2 * t + 1, 16, stride=8), :] = jnp.where(first_half, pltpu.roll(even, 64, 1), odd)
 
 
-def list_atoms(owner, anchor, gz):
+def list_atoms(owner, anchor, extent, gz):
     rank = owner[...]
     z = jnp.concatenate([anchor[2:3, 128 * r : 128 * r + 128] for r in range(8)], axis=0)
     slab = rank % 8
@@ -347,29 +367,30 @@
 
     at_own, n_own = ranks(own)
     at_near, n_near = ranks(near)
-    first = jnp.floor((n_own + 7.0) * 0.125) * 8.0
-    last = first + jnp.floor((n_near + 7.0) * 0.125) * 8.0
+    first = jnp.floor((n_own + (GROUP - 1.0)) * (1.0 / GROUP)) * GROUP
+    last = first + jnp.floor((n_near + (GROUP - 1.0)) * (1.0 / GROUP)) * GROUP
     at = jnp.where(own, at_own, jnp.where(near, at_near + first, -1.0)).astype(jnp.int32)
     high = jnp.where(at >= 0, at // 128, -1)
     low = (at % 128).astype(F32).T
     ident = 128 * sub + lax.broadcasted_iota(jnp.int32, (8, 128), 1) + 1
     slot_row = lax.broadcasted_iota(jnp.int32, (16, 128), 0)
-    big = jnp.zeros((16, 128), F32)
-    small = jnp.zeros((16, 128), F32)
+    shift = jnp.where(near, jnp.where(slab == (gz + 1) % 8, 128, -128), 0)
+    fields = [ident // 32, ident % 32, rank // 8, z + shift + PAD, extent[...]]
+    found = jnp.zeros((80, 128), F32)
     for r in range(8):
         hit = slot_row == high[r : r + 1]
         right = (low[:, r : r + 1] == col.astype(F32)).astype(BF16)
-        one = ident[r : r + 1]
-        big = big + jnp.dot(jnp.where(hit, (one // 32).astype(F32), 0.0).astype(BF16), right, preferred_element_type=F32)
-        small = small + jnp.dot(jnp.where(hit, (one % 32).astype(F32), 0.0).astype(BF16), right, preferred_element_type=F32)
-    table = big * 32.0 + small
+        left = [jnp.where(hit, f[r : r + 1].astype(F32), 0.0).astype(BF16) for f in fields]
+        found = found + jnp.dot(jnp.concatenate(left, axis=0), right, preferred_element_type=F32)
+    table = found[:16] * 32.0 + found[16:32]
     lane = lax.broadcasted_iota(jnp.int32, (16, 128), 1)
+    start = jnp.where(table > 0.0, found[48:64], float(PAD))
     table = jnp.where(slot_row == 15, jnp.where(lane == 0, first, jnp.where(lane == 1, last, 0.0)), table)
-    return table.astype(jnp.int32)
+    return jnp.concatenate([table, found[32:48], start, found[64:80]], axis=0).astype(jnp.int32)
 
 
 def gather_kernel(
-    orb, pot, proj, perm, owner, anchor, x_out, v_out, p_out, table,
+    orb, pot, proj, perm, owner, anchor, extent, x_out, v_out, p_out, table,
     sent, vown, pown, cells, pair,
     a2a_send, a2a_recv, p_send, p_recv, v_send, v_recv, twin_send, twin_recv, halo_send, halo_recv, here,
 ):
@@ -409,7 +430,7 @@
         idx[dim] = at
         return v_out.at[idx[0], idx[1], pl.ds(16 + start, rows)]
 
-    used = [0, 0, 0]
+    used = [0] * len(PARTS)
 
     def p_copy(part, src, dim, step):
         k = used[part]
@@ -448,19 +469,14 @@
 
         lax.fori_loop(lo_o, hi_o, step, 0)
 
-    def v_copies(phase, second):
+    def v_copies(phase):
         out = []
         for i, (at, rows, half, order) in enumerate(V_PARTS):
             dim, held = order[phase], order[:phase]
-            base = 4 * phase
-            if not second:
-                own = v_view(held, dim, where[dim], at, rows)
-                for k, step in ((0, 1), (1, -1)):
-                    out.append(remote(own, own, v_send.at[i, base + k], v_recv.at[i, base + k], neighbour(dim, step)))
-            else:
-                for k, step, lo_r, n_r in ((2, 1, 0, half), (3, -1, half, rows - half)):
-                    src = v_view(held, dim, near(dim, -step), at + lo_r, n_r)
-                    out.append(remote(src, src, v_send.at[i, base + k], v_recv.at[i, base + k], neighbour(dim, step)))
+            src = v_view(held, dim, where[dim], at, rows)
+            for k in range(3):
+                sems = (v_send.at[i, 3 * phase + k], v_recv.at[i, 3 * phase + k])
+                out.append(remote(src, src, *sems, neighbour(dim, k + 1)))
         return out
 
     def along3(part, at2):
@@ -475,95 +491,51 @@
             p_copy(part, p_view(part, at2, near(d3, 1), (half, rows - half)), d3, -1),
         ]
 
-    three = range(3)
+    every = range(len(PARTS))
     dims = [part[3] for part in PARTS]
+    right, left = line_peer(1), line_peer(7)
+    whole = pl.ds(0, 4)
     wait(local)
 
-    m1 = []
-    for i in three:
+    first = []
+    for i in every:
         d1, d2, d3 = dims[i]
         own = p_view(i, where[d2], where[d3], (0, PARTS[i][1]), where[d1])
-        m1 += [p_copy(i, own, d1, 1), p_copy(i, own, d1, -1)]
-    start(m1)
-    v = start(v_copies(0, False))
-    send_a2a(1, 4)
-    wait(m1)
-    m2 = []
-    for i in three:
-        d1, d2, d3 = dims[i]
-        rows, half = PARTS[i][1], PARTS[i][2]
-        m2 += [
-            p_copy(i, p_view(i, where[d2], where[d3], (0, half), near(d1, -1)), d1, 1),
-            p_copy(i, p_view(i, where[d2], where[d3], (half, rows - half), near(d1, 1)), d1, -1),
-        ]
-    start(m2)
-    wait(v)
-    v = start(v_copies(0, True))
-    send_a2a(4, 7)
-    wait(m2)
-    s3 = []
-    for i in three:
+        first += [p_copy(i, own, d1, k) for k in (1, 2, 3)]
+    start(first)
+    v = start(v_copies(0))
+    send_a2a(1, A2A_CUTS[0])
+    wait(first)
+    second, a5 = [], []
+    for i in every:
         d1, d2, d3 = dims[i]
         row = p_view(i, where[d2], where[d3], (0, PARTS[i][1]))
-        s3 += [p_copy(i, row, d2, 1), p_copy(i, row, d2, -1)]
-    start(s3)
-    a5 = start([c for i in three for c in along3(i, where[dims[i][1]])])
-    for i in three:
-        twin(i, where[dims[i][1]], where[dims[i][2]])
+        second += [p_copy(i, row, d2, k) for k in (1, 2, 3)]
+    start(second)
+    for i in every:
+        a5 += start(along3(i, where[dims[i][1]]))
     wait(v)
-    v = start(v_copies(1, False))
-    send_a2a(7, 10)
-    wait(s3)
-    s4 = []
-    for i in three:
-        d1, d2, d3 = dims[i]
-        rows, half = PARTS[i][1], PARTS[i][2]
-        s4 += [
-            p_copy(i, p_view(i, near(d2, -1), where[d3], (0, half)), d2, 1),
-            p_copy(i, p_view(i, near(d2, 1), where[d3], (half, rows - half)), d2, -1),
-        ]
-    start(s4)
-    b5 = start([c for i in three for k in (1, -1) for c in along3(i, near(dims[i][1], k))])
-    for i in three:
-        for k in (1, -1):
-            twin(i, near(dims[i][1], k), where[dims[i][2]])
+    v = start(v_copies(1))
+    send_a2a(A2A_CUTS[0], A2A_CUTS[1])
+    wait(second)
+    b5 = []
+    for i in every:
+        for k in (1, 2, 3):
+            b5 += start(along3(i, near(dims[i][1], k)))
+    for i in every:
+        twin(i, whole, where[dims[i][2]])
     wait(v)
-    v = start(v_copies(1, True))
-    wait(a5)
-    a6 = start([c for i in three for c in forward3(i, where[dims[i][1]])])
-    for i in three:
-        for k in (1, -1):
-            twin(i, where[dims[i][1]], near(dims[i][2], k))
-    send_a2a(10, 13)
-    wait(s4)
-    c5 = start([c for i in three for c in along3(i, near(dims[i][1], 2))])
-    for i in three:
-        twin(i, near(dims[i][1], 2), where[dims[i][2]])
-    send_a2a(13, 16)
-    wait(v)
-    right, left = line_peer(1), line_peer(7)
-    whole = pl.ds(0, 4)
     halos = start([
         remote(v_out.at[whole, whole, pl.ds(64, 16)], v_out.at[whole, whole, pl.ds(0, 16)],
                halo_send.at[2], halo_recv.at[2], right),
         remote(v_out.at[whole, whole, pl.ds(16, 16)], v_out.at[whole, whole, pl.ds(80, 16)],
                halo_send.at[3], halo_recv.at[3], left),
     ])
-    wait(b5)
-    b6 = start([c for i in three for k in (1, -1) for c in forward3(i, near(dims[i][1], k))])
-    for i in three:
-        for m in (1, -1):
-            for k in (1, -1):
-                twin(i, near(dims[i][1], m), near(dims[i][2], k))
-    table[...] = list_atoms(owner, anchor, gz)
-    wait(a6)
-    for i in three:
-        twin(i, where[dims[i][1]], near(dims[i][2], 2))
-    wait(c5)
-    c6 = start([c for i in three for c in forward3(i, near(dims[i][1], 2))])
-    for i in three:
-        for k in (1, -1):
-            twin(i, near(dims[i][1], 2), near(dims[i][2], k))
+    wait(a5)
+    last = []
+    for i in every:
+        last += start(forward3(i, where[dims[i][1]]))
+    table[...] = list_atoms(owner, anchor, extent, gz)
 
     def finish_a2a(o, _):
         a2a(o).wait()
@@ -576,13 +548,16 @@
         remote(x_out.at[pl.ds(0, G), pl.ds(PAD, HALO)], x_out.at[pl.ds(0, G), pl.ds(PAD + 128, HALO)],
                halo_send.at[1], halo_recv.at[1], left),
     ])
-    wait(b6)
-    for i in three:
+    wait(b5)
+    for i in every:
+        for k in (1, 2, 3):
+            last += start(forward3(i, near(dims[i][1], k)))
+    for i in every:
         for k in (1, -1):
-            twin(i, near(dims[i][1], k), near(dims[i][2], 2))
-    wait(c6)
-    for i in three:
-        twin(i, near(dims[i][1], 2), near(dims[i][2], 2))
+            twin(i, whole, near(dims[i][2], k))
+    wait(last)
+    for i in every:
+        twin(i, whole, near(dims[i][2], 2))
     wait(halos)
     wait([copy for _, copy in twins])
 
@@ -594,7 +569,7 @@
     return perm
 
 
-def run_gather(orb, pot, proj, perm, owner, anchor):
+def run_gather(orb, pot, proj, perm, owner, anchor, extent):
     vmem = pl.BlockSpec(memory_space=pltpu.VMEM)
     hbm = pl.BlockSpec(memory_space=pltpu.HBM)
     dma = pltpu.SemaphoreType.DMA
@@ -604,9 +579,9 @@
             jax.ShapeDtypeStruct((G, ROWS, 128), F32),
             jax.ShapeDtypeStruct((4, 4, 96, 128), F32),
             jax.ShapeDtypeStruct((4, 4, 4, 2, 128, 128), F32),
-            jax.ShapeDtypeStruct((16, 128), jnp.int32),
+            jax.ShapeDtypeStruct((64, 128), jnp.int32),
         ),
-        in_specs=[vmem] * 6,
+        in_specs=[vmem] * 7,
         out_specs=(hbm, hbm, hbm, vmem),
         scratch_shapes=[
             pltpu.VMEM((G, 128, 128), F32),
@@ -614,12 +589,12 @@
             pltpu.VMEM((128, 128), F32),
             pltpu.VMEM((4, 32, 128), F32),
             pltpu.VMEM((128, 64), F32),
-            dma((16,)), dma((16,)), dma((3, 24)), dma((3, 24)), dma((2, 8)), dma((2, 8)),
-            dma((3, 16)), dma((3, 16)), dma((4,)), dma((4,)), dma((3,)),
+            dma((16,)), dma((16,)), dma((4, 22)), dma((4, 22)), dma((2, 6)), dma((2, 6)),
+            dma((4, 4)), dma((4, 4)), dma((4,)), dma((4,)), dma((3,)),
         ],
         compiler_params=pltpu.CompilerParams(collective_id=1, has_side_effects=True),
         name="gather",
-    )(orb, pot, proj, perm, owner, anchor)
+    )(orb, pot, proj, perm, owner, anchor, extent)
 
 
 def return_kernel(
@@ -728,12 +703,12 @@
 def body(orbitals, potential, projectors, owner_rank, box_anchor, box_extent, coupling):
     perm = jnp.asarray(permutation()).astype(BF16)
     x, v, p, table = run_gather(
-        orbitals.reshape(2048, 128), potential.reshape(64, 128), projectors.reshape(32, 512), perm,
-        owner_rank.reshape(8, 128), box_anchor,
+        orbitals.reshape(2048, 128), potential.reshape(64, 128), projectors, perm,
+        owner_rank.reshape(8, 128), box_anchor, box_extent.reshape(8, 128),
     )
     w = jnp.asarray(weights()).astype(BF16)
     y = run_filter(
-        table, owner_rank, box_anchor, box_extent, coupling.T,
+        table, coupling.T,
         x, v.reshape(G, 96, 128), p.reshape(1024, 16, 128), w,
     )
     filtered, total = run_return(y)

time: 129 us -> 116 us (0.90)
  Pallas kernels: 122 us -> 111 us
  local copies, waits for them, and re-layouts: 5.12 us -> 3.63 us
    pallas_call x1, Pallas kernels: 31.7 us -> 25.7 us  [run_filter(): pl.pallas_call(filter_kernel, out_shape=jax.ShapeDtypeStruct((G, 128, 128...]
    pallas_call x1, Pallas kernels: 37.6 us -> 33.2 us  [run_return(): pl.pallas_call(return_kernel, out_shape=(jax.ShapeDtypeStruct((2048, 128)...]
    reshape x1 -> x0, local copies, waits for them, and re-layouts: 1.49 us -> none  [body(): projectors.reshape(32, 512)]
where the time goes in v4:
time: 116 us; the launch traced here: 115 us
  Pallas kernels  111 us (96%)
  local copies, waits for them, and re-layouts  3.63 us (3%)
    pallas_call x1, Pallas kernels, run_gather(): pl.pallas_call(gather_kernel, out_shape=(jax.ShapeDtypeStruct((G, ROWS, 1...  51.6 us
    pallas_call x1, Pallas kernels, run_return(): pl.pallas_call(return_kernel, out_shape=(jax.ShapeDtypeStruct((2048, 128)...  33.2 us
    pallas_call x1, Pallas kernels, run_filter(): pl.pallas_call(filter_kernel, out_shape=jax.ShapeDtypeStruct((G, 128, 128...  25.7 us
    unnamed x2, local copies, waits for them, and re-layouts  3.63 us

profile of v4, /device:TPU:1, one launch (start us, length us, event | category | flops | bytes accessed | tf_op | source)
XLA Modules:
  0.0 114.8 jit_solution(373911473185767837)
XLA Ops:
  0.6 51.6 %gather.1 = (f32[16,208,128]{2,1,0:T(8,128)}, f32[4,4,96,128]{3,2,1,0:T(8,128)}, f32[4,4,4,2,128,128]{5,4,3,2,1,0:T(8,128)}, s32[64,128]{1,0:T(8,128)}) custom-call(f32[2048,128]{1,0:T(8,128)} %bitcast.9, f32[64,128]{1,0:T(8,128)} %bitcast.12, f32[8,4,512]{2,1,0:T(4,128)} %proj.1, bf16[512,512]{1,0:T(8,128)(2,1)} %constant.7.perm, s32[8,128]{1,0:T(8,128)} %bitcast.14, ...), custom_call_target="tpu_custom_call" | custom-call | tf_op jit(solution)/shard_map/gather/pallas_call | solution.py:576
  52.2 25.7 %chebyshev.1.y = f32[16,128,128]{2,1,0:T(8,128)} custom-call(s32[64,128]{1,0:T(8,128)} %get-tuple-element.8.table, f32[4,1024]{1,0:T(4,128)} %bitcast.13, f32[16,208,128]{2,1,0:T(8,128)} %get-tuple-element.9.x_ref, f32[16,96,128]{2,1,0:T(8,128)} %bitcast.11, f32[1024,16,128]{2,1,0:T(8,128)} %bitcast.8, bf16[1536,256]{1,0:T(8,128)(2,1)} %constant.8.w_ref), custom_call_target="tpu_custom_call" | custom-call | tf_op jit(solution)/shard_map/chebyshev/pallas_call | solution.py:255
  77.9 33.2 %giveback.1 = (f32[2048,128]{1,0:T(8,128)}, f32[32,32]{1,0:T(8,128)}) custom-call(f32[16,128,128]{2,1,0:T(8,128)} %chebyshev.1.y), custom_call_target="tpu_custom_call" | custom-call | tf_op jit(solution)/shard_map/giveback/pallas_call | solution.py:687
  111.2 2.3 %copy.13 = f32[32,8,8,128]{3,2,1,0:T(8,128)} copy(f32[32,8,8,128]{3,2,1,0:T(8,128)} %bitcast.10) | data formatting | bytes 2097152
  113.5 1.3 %copy.14 = f32[32,32]{1,0:T(8,128)} copy(f32[32,32]{1,0:T(8,128)} %get-tuple-element.17) | data formatting | bytes 8192

commit v5 on v4

--- a/solution.py
+++ b/solution.py
@@ -278,7 +278,7 @@
 
 MESH = pl.DeviceIdType.MESH
 PARTS = ((0, 24, 16, (0, 1, 2)), (24, 24, 16, (1, 0, 2)), (48, 40, 24, (1, 2, 0)), (88, 40, 24, (0, 2, 1)))
-A2A_CUTS = (9, 16)
+A2A_CUTS = (12, 16)
 V_PARTS = ((0, 32, 16, (0, 1)), (32, 32, 16, (1, 0)))
 
 
@@ -432,10 +432,10 @@
 
     used = [0] * len(PARTS)
 
-    def p_copy(part, src, dim, step):
+    def p_copy(part, src, dim, step, dst=None):
         k = used[part]
         used[part] += 1
-        return remote(src, src, p_send.at[part, k], p_recv.at[part, k], neighbour(dim, step))
+        return remote(src, src if dst is None else dst, p_send.at[part, k], p_recv.at[part, k], neighbour(dim, step))
 
     partner = (gx, gy, gz + 1 - 2 * core)
     twins = []
@@ -473,10 +473,11 @@
         out = []
         for i, (at, rows, half, order) in enumerate(V_PARTS):
             dim, held = order[phase], order[:phase]
-            src = v_view(held, dim, where[dim], at, rows)
+            dst = v_view(held, dim, where[dim], at, rows)
+            src = dst if phase else vown.at[pl.ds(at, rows)]
             for k in range(3):
                 sems = (v_send.at[i, 3 * phase + k], v_recv.at[i, 3 * phase + k])
-                out.append(remote(src, src, *sems, neighbour(dim, k + 1)))
+                out.append(remote(src, dst, *sems, neighbour(dim, k + 1)))
         return out
 
     def along3(part, at2):
@@ -495,33 +496,36 @@
     dims = [part[3] for part in PARTS]
     right, left = line_peer(1), line_peer(7)
     whole = pl.ds(0, 4)
-    wait(local)
-
     first = []
     for i in every:
         d1, d2, d3 = dims[i]
         own = p_view(i, where[d2], where[d3], (0, PARTS[i][1]), where[d1])
-        first += [p_copy(i, own, d1, k) for k in (1, 2, 3)]
+        src = pown.at[pl.ds(PARTS[i][0], PARTS[i][1])]
+        first += [p_copy(i, src, d1, k, own) for k in (1, 3, 2)]
     start(first)
     v = start(v_copies(0))
     send_a2a(1, A2A_CUTS[0])
+    table[...] = list_atoms(owner, anchor, extent, gz)
+    wait(local)
     wait(first)
     second, a5 = [], []
-    for i in every:
-        d1, d2, d3 = dims[i]
-        row = p_view(i, where[d2], where[d3], (0, PARTS[i][1]))
-        second += [p_copy(i, row, d2, k) for k in (1, 2, 3)]
+    for k in (1, 3, 2):
+        for i in every:
+            d1, d2, d3 = dims[i]
+            second.append(p_copy(i, p_view(i, where[d2], where[d3], (0, PARTS[i][1])), d2, k))
     start(second)
     for i in every:
         a5 += start(along3(i, where[dims[i][1]]))
     wait(v)
     v = start(v_copies(1))
     send_a2a(A2A_CUTS[0], A2A_CUTS[1])
-    wait(second)
     b5 = []
-    for i in every:
-        for k in (1, 2, 3):
-            b5 += start(along3(i, near(dims[i][1], k)))
+    at = 0
+    for k in (1, 3, 2):
+        for i in every:
+            wait(second[at : at + 1])
+            at += 1
+            b5 += start(along3(i, near(dims[i][1], -k)))
     for i in every:
         twin(i, whole, where[dims[i][2]])
     wait(v)
@@ -535,12 +539,17 @@
     last = []
     for i in every:
         last += start(forward3(i, where[dims[i][1]]))
-    table[...] = list_atoms(owner, anchor, extent, gz)
 
     def finish_a2a(o, _):
         a2a(o).wait()
         return 0
 
+    at = 0
+    for k in (1, 3, 2):
+        for i in every:
+            wait(b5[at : at + 2])
+            at += 2
+            last += start(forward3(i, near(dims[i][1], -k)))
     lax.fori_loop(1, 16, finish_a2a, 0)
     halos += start([
         remote(x_out.at[pl.ds(0, G), pl.ds(PAD + 128 - HALO, HALO)], x_out.at[pl.ds(0, G), pl.ds(PAD - HALO, HALO)],
@@ -548,10 +557,6 @@
         remote(x_out.at[pl.ds(0, G), pl.ds(PAD, HALO)], x_out.at[pl.ds(0, G), pl.ds(PAD + 128, HALO)],
                halo_send.at[1], halo_recv.at[1], left),
     ])
-    wait(b5)
-    for i in every:
-        for k in (1, 2, 3):
-            last += start(forward3(i, near(dims[i][1], k)))
     for i in every:
         for k in (1, -1):
             twin(i, whole, near(dims[i][2], k))
@@ -687,7 +692,7 @@
     return pl.pallas_call(
         return_kernel,
         out_shape=(jax.ShapeDtypeStruct((2048, 128), F32), jax.ShapeDtypeStruct((32, 32), F32)),
-        in_specs=[vmem],
+        in_specs=[pl.BlockSpec(memory_space=pltpu.HBM)],
         out_specs=(vmem, vmem),
         scratch_shapes=[
             pltpu.VMEM((G, 128, 128), F32),

time: 116 us -> 111 us (0.957); the launches traced: 115 us -> 112 us
  Pallas kernels: 111 us -> 108 us
    pallas_call x1, Pallas kernels: 51.6 us -> 48.5 us  [run_gather(): pl.pallas_call(gather_kernel, out_shape=(jax.ShapeDtypeStruct((G, ROWS, 1...]
where the time goes in v5:
time: 111 us; the launch traced here: 112 us
  Pallas kernels  108 us (97%)
  local copies, waits for them, and re-layouts  3.63 us (3%)
    pallas_call x1, Pallas kernels, run_gather(): pl.pallas_call(gather_kernel, out_shape=(jax.ShapeDtypeStruct((G, ROWS, 1...  48.5 us
    pallas_call x1, Pallas kernels, run_return(): pl.pallas_call(return_kernel, out_shape=(jax.ShapeDtypeStruct((2048, 128)...  33.4 us
    pallas_call x1, Pallas kernels, run_filter(): pl.pallas_call(filter_kernel, out_shape=jax.ShapeDtypeStruct((G, 128, 128...  25.6 us
    unnamed x2, local copies, waits for them, and re-layouts  3.63 us

profile of v5, /device:TPU:1, one launch (start us, length us, event | category | flops | bytes accessed | tf_op | source)
XLA Modules:
  0.0 111.9 jit_solution(18305825182273368319)
XLA Ops:
  0.6 48.5 %gather.1 = (f32[16,208,128]{2,1,0:T(8,128)}, f32[4,4,96,128]{3,2,1,0:T(8,128)}, f32[4,4,4,2,128,128]{5,4,3,2,1,0:T(8,128)}, s32[64,128]{1,0:T(8,128)}) custom-call(f32[2048,128]{1,0:T(8,128)} %bitcast.9, f32[64,128]{1,0:T(8,128)} %bitcast.12, f32[8,4,512]{2,1,0:T(4,128)} %proj.1, bf16[512,512]{1,0:T(8,128)(2,1)} %constant.7.perm, s32[8,128]{1,0:T(8,128)} %bitcast.14, ...), custom_call_target="tpu_custom_call" | custom-call | tf_op jit(solution)/shard_map/gather/pallas_call | solution.py:581
  49.2 25.6 %chebyshev.1.y = f32[16,128,128]{2,1,0:T(8,128)} custom-call(s32[64,128]{1,0:T(8,128)} %get-tuple-element.8.table, f32[4,1024]{1,0:T(4,128)} %bitcast.13, f32[16,208,128]{2,1,0:T(8,128)} %get-tuple-element.9.x_ref, f32[16,96,128]{2,1,0:T(8,128)} %bitcast.11, f32[1024,16,128]{2,1,0:T(8,128)} %bitcast.8, bf16[1536,256]{1,0:T(8,128)(2,1)} %constant.8.w_ref), custom_call_target="tpu_custom_call" | custom-call | tf_op jit(solution)/shard_map/chebyshev/pallas_call | solution.py:255
  74.8 33.4 %giveback.1 = (f32[2048,128]{1,0:T(8,128)}, f32[32,32]{1,0:T(8,128)}) custom-call(f32[16,128,128]{2,1,0:T(8,128)} %chebyshev.1.y), custom_call_target="tpu_custom_call" | custom-call | tf_op jit(solution)/shard_map/giveback/pallas_call | solution.py:692
  108.2 2.3 %copy.13 = f32[32,8,8,128]{3,2,1,0:T(8,128)} copy(f32[32,8,8,128]{3,2,1,0:T(8,128)} %bitcast.10) | data formatting | bytes 2097152
  110.5 1.3 %copy.14 = f32[32,32]{1,0:T(8,128)} copy(f32[32,32]{1,0:T(8,128)} %get-tuple-element.17) | data formatting | bytes 8192

commit v6 on v5

--- a/solution.py
+++ b/solution.py
@@ -278,6 +278,7 @@
 
 MESH = pl.DeviceIdType.MESH
 PARTS = ((0, 24, 16, (0, 1, 2)), (24, 24, 16, (1, 0, 2)), (48, 40, 24, (1, 2, 0)), (88, 40, 24, (0, 2, 1)))
+FAR_FIRST = (10, 6, 9, 11, 14, 5, 7, 13, 15, 2, 8, 1, 3, 4, 12)
 A2A_CUTS = (12, 16)
 V_PARTS = ((0, 32, 16, (0, 1)), (32, 32, 16, (1, 0)))
 
@@ -618,11 +619,8 @@
             y.at[4 * peer[0] + peer[1]], recv.at[mine], a2a_send.at[o], a2a_recv.at[o], peer
         )
 
-    def send(o, _):
+    for o in FAR_FIRST:
         a2a(o).start()
-        return 0
-
-    lax.fori_loop(1, 16, send, 0)
 
     def place(source):
         out[pl.ds(pl.multiple_of(128 * source, 128), 128), :] = recv[source].T
@@ -654,29 +652,23 @@
     def line(o):
         return remote(gram_b.at[gz], gram_b.at[gz], b_send.at[o], b_recv.at[o], line_peer(o))
 
-    def start_plane(o, _):
-        plane(o).start()
-        return 0
-
     def wait_plane(o, _):
         plane(o).wait()
         return 0
 
-    def start_line(o, _):
-        line(o).start()
-        return 0
-
     def wait_line(o, _):
         line(o).wait()
         return 0
 
-    lax.fori_loop(1, 16, start_plane, 0)
+    for o in FAR_FIRST:
+        plane(o).start()
     lax.fori_loop(1, 16, wait_plane, 0)
     acc = gram_a[0]
     for i in range(1, 16):
         acc = acc + gram_a[i]
     gram_b[gz] = acc
-    lax.fori_loop(1, 8, start_line, 0)
+    for o in (4, 3, 5, 2, 6, 1, 7):
+        line(o).start()
     lax.fori_loop(1, 8, wait_line, 0)
     acc = gram_b[0]
     for i in range(1, 8):

time: 111 us -> 110 us (level)
  Pallas kernels: 108 us -> 106 us
    pallas_call x1, Pallas kernels: 33.4 us -> 31.7 us  [run_return(): pl.pallas_call(return_kernel, out_shape=(jax.ShapeDtypeStruct((2048, 128)...]
where the time goes in v6:
time: 110 us
  Pallas kernels  106 us (96%)
  local copies, waits for them, and re-layouts  3.63 us (3%)
    pallas_call x1, Pallas kernels, run_gather(): pl.pallas_call(gather_kernel, out_shape=(jax.ShapeDtypeStruct((G, ROWS, 1...  48.5 us
    pallas_call x1, Pallas kernels, run_return(): pl.pallas_call(return_kernel, out_shape=(jax.ShapeDtypeStruct((2048, 128)...  31.7 us
    pallas_call x1, Pallas kernels, run_filter(): pl.pallas_call(filter_kernel, out_shape=jax.ShapeDtypeStruct((G, 128, 128...  25.6 us
    unnamed x2, local copies, waits for them, and re-layouts  3.63 us

profile of v6, /device:TPU:1, one launch (start us, length us, event | category | flops | bytes accessed | tf_op | source)
XLA Modules:
  0.0 110.2 jit_solution(6046570584667187281)
XLA Ops:
  0.6 48.5 %gather.1 = (f32[16,208,128]{2,1,0:T(8,128)}, f32[4,4,96,128]{3,2,1,0:T(8,128)}, f32[4,4,4,2,128,128]{5,4,3,2,1,0:T(8,128)}, s32[64,128]{1,0:T(8,128)}) custom-call(f32[2048,128]{1,0:T(8,128)} %bitcast.9, f32[64,128]{1,0:T(8,128)} %bitcast.12, f32[8,4,512]{2,1,0:T(4,128)} %proj.1, bf16[512,512]{1,0:T(8,128)(2,1)} %constant.7.perm, s32[8,128]{1,0:T(8,128)} %bitcast.14, ...), custom_call_target="tpu_custom_call" | custom-call | tf_op jit(solution)/shard_map/gather/pallas_call | solution.py:582
  49.2 25.6 %chebyshev.1.y = f32[16,128,128]{2,1,0:T(8,128)} custom-call(s32[64,128]{1,0:T(8,128)} %get-tuple-element.8.table, f32[4,1024]{1,0:T(4,128)} %bitcast.13, f32[16,208,128]{2,1,0:T(8,128)} %get-tuple-element.9.x_ref, f32[16,96,128]{2,1,0:T(8,128)} %bitcast.11, f32[1024,16,128]{2,1,0:T(8,128)} %bitcast.8, bf16[1536,256]{1,0:T(8,128)(2,1)} %constant.8.w_ref), custom_call_target="tpu_custom_call" | custom-call | tf_op jit(solution)/shard_map/chebyshev/pallas_call | solution.py:255
  74.8 31.7 %giveback.1 = (f32[2048,128]{1,0:T(8,128)}, f32[32,32]{1,0:T(8,128)}) custom-call(f32[16,128,128]{2,1,0:T(8,128)} %chebyshev.1.y), custom_call_target="tpu_custom_call" | custom-call | tf_op jit(solution)/shard_map/giveback/pallas_call | solution.py:684
  106.5 2.3 %copy.13 = f32[32,8,8,128]{3,2,1,0:T(8,128)} copy(f32[32,8,8,128]{3,2,1,0:T(8,128)} %bitcast.10) | data formatting | bytes 2097152
  108.8 1.3 %copy.14 = f32[32,32]{1,0:T(8,128)} copy(f32[32,32]{1,0:T(8,128)} %get-tuple-element.17) | data formatting | bytes 8192

commit v7 on v6

--- a/solution.py
+++ b/solution.py
@@ -673,7 +673,6 @@
     acc = gram_b[0]
     for i in range(1, 8):
         acc = acc + gram_b[i]
-    acc = acc * (1.0 / (32 * 32 * 1024))
     for b in range(4):
         total[pl.ds(8 * b, 8), :] = acc[:, 32 * b : 32 * b + 32]
 
@@ -709,7 +708,7 @@
         x, v.reshape(G, 96, 128), p.reshape(1024, 16, 128), w,
     )
     filtered, total = run_return(y)
-    return filtered.reshape(orbitals.shape), total
+    return filtered.reshape(orbitals.shape), total * (1.0 / (32 * 32 * 1024))
 
 
 def solution(mesh):

time: 110 us -> 111 us (level)
  other arithmetic: 0 us -> 1.33 us
  local copies, waits for them, and re-layouts: 3.63 us -> 2.31 us
    mul x0 -> x1, other arithmetic: none -> 1.33 us  [body(): return (filtered.reshape(orbitals.shape), total * (1.0 / (32 * 32 * 1024)))]
    unnamed x2 -> x1, local copies, waits for them, and re-layouts: 3.63 us -> 2.31 us
    pallas_call x1, Pallas kernels: 31.7 us -> 32.9 us  [run_return(): pl.pallas_call(return_kernel, out_shape=(jax.ShapeDtypeStruct((2048, 128)...]
where the time goes in v7:
time: 111 us; the launch traced here: 110 us
  Pallas kernels  106 us (95%)
  local copies, waits for them, and re-layouts  2.31 us (2%)
  other arithmetic  1.33 us (1%)
    pallas_call x1, Pallas kernels, run_gather(): pl.pallas_call(gather_kernel, out_shape=(jax.ShapeDtypeStruct((G, ROWS, 1...  48.5 us
    pallas_call x1, Pallas kernels, run_return(): pl.pallas_call(return_kernel, out_shape=(jax.ShapeDtypeStruct((2048, 128)...  32.9 us
    pallas_call x1, Pallas kernels, run_filter(): pl.pallas_call(filter_kernel, out_shape=jax.ShapeDtypeStruct((G, 128, 128...  24.7 us
    unnamed x1, local copies, waits for them, and re-layouts  2.31 us

profile of v7, /device:TPU:1, one launch (start us, length us, event | category | flops | bytes accessed | tf_op | source)
XLA Modules:
  0.0 110.5 jit_solution(2302345034324128672)
XLA Ops:
  0.6 48.5 %gather.1 = (f32[16,208,128]{2,1,0:T(8,128)}, f32[4,4,96,128]{3,2,1,0:T(8,128)}, f32[4,4,4,2,128,128]{5,4,3,2,1,0:T(8,128)}, s32[64,128]{1,0:T(8,128)}) custom-call(f32[2048,128]{1,0:T(8,128)} %bitcast.9, f32[64,128]{1,0:T(8,128)} %bitcast.12, f32[8,4,512]{2,1,0:T(4,128)} %proj.1, bf16[512,512]{1,0:T(8,128)(2,1)} %constant.9.perm, s32[8,128]{1,0:T(8,128)} %bitcast.14, ...), custom_call_target="tpu_custom_call" | custom-call | tf_op jit(solution)/shard_map/gather/pallas_call | solution.py:582
  49.2 24.7 %chebyshev.1.y = f32[16,128,128]{2,1,0:T(8,128)} custom-call(s32[64,128]{1,0:T(8,128)} %get-tuple-element.8.table, f32[4,1024]{1,0:T(4,128)} %bitcast.13, f32[16,208,128]{2,1,0:T(8,128)} %get-tuple-element.9.x_ref, f32[16,96,128]{2,1,0:T(8,128)} %bitcast.11, f32[1024,16,128]{2,1,0:T(8,128)} %bitcast.8, bf16[1536,256]{1,0:T(8,128)(2,1)} %constant.10.w_ref), custom_call_target="tpu_custom_call" | custom-call | tf_op jit(solution)/shard_map/chebyshev/pallas_call | solution.py:255
  73.9 32.9 %giveback.1 = (f32[2048,128]{1,0:T(8,128)}, f32[32,32]{1,0:T(8,128)}) custom-call(f32[16,128,128]{2,1,0:T(8,128)} %chebyshev.1.y), custom_call_target="tpu_custom_call" | custom-call | tf_op jit(solution)/shard_map/giveback/pallas_call | solution.py:683
  106.8 1.3 %broadcast_multiply_fusion = f32[32,32]{1,0:T(8,128)} fusion(f32[32,32]{1,0:T(8,128)} %get-tuple-element.13), kind=kLoop, calls=%fused_computation | loop fusion | flops 1024 | bytes 8192 | tf_op jit(solution)/shard_map/mul | solution.py:711
  108.2 2.3 %copy.12 = f32[32,8,8,128]{3,2,1,0:T(8,128)} copy(f32[32,8,8,128]{3,2,1,0:T(8,128)} %bitcast.10) | data formatting | bytes 2097152
